TPU v7x, 256 devices: a whole 4x4x8 slice. The times are simulated.
256 devices in a mesh: row: 16 (over x, y_hi, core), col: 16 (over z, y_lo).
Axes of the slice: x: 4, y: 4 (y_hi: 2, y_lo: 2; y = y_hi * 2 + y_lo), z: 8, core: 2. Of those that a mesh axis runs over, the one named last changes fastest.
Arguments:
- image: float32 [2048, 2048], P('row', 'col'), may hold values from -10.1 to 10.1
Outputs:
- features: bfloat16 [12, 2048, 2048], P(None, 'row', 'col')
All inputs are finite; a program needn't handle non-finite values.
Results may differ from a plain program's by a relative error of at most 0.0014.
Values sent between devices are 32-bit elements; how exact they have to be, the bound alone decides.
A program may use at most 64 MiB of HBM per device.

v0:
```python
import math

import jax
import jax.numpy as jnp
import numpy as np
from jax import lax
from jax.sharding import PartitionSpec as P

SIG_A = 128
SIG_B = 256


DER_FIRST = (
    1.0 / 280,
    -4.0 / 105,
    1.0 / 5,
    -4.0 / 5,
    0.0,
    4.0 / 5,
    -1.0 / 5,
    4.0 / 105,
    -1.0 / 280,
)
DER_SECOND = (
    -1.0 / 560,
    8.0 / 315,
    -1.0 / 5,
    8.0 / 5,
    -205.0 / 72,
    8.0 / 5,
    -1.0 / 5,
    8.0 / 315,
    -1.0 / 560,
)
DERICHE_POLES = ((1.68, 3.735, 1.783, 0.6318), (-0.6803, -0.2598, 1.723, 1.997))
HIGHEST = lax.Precision.HIGHEST


def passed_along(value, axis, steps):
    count = lax.axis_size(axis)
    leading, last = (max(0, -steps), min(count, count - steps))
    return lax.ppermute(value, axis, [(source, source + steps) for source in range(leading, last)])


def extended(block, sides, width):
    for axis, dim in sides:
        count = lax.axis_size(axis)
        forward = [(i, i + 1) for i in range(count - 1)]
        backward = [(target, source) for source, target in forward]
        low = lax.ppermute(
            lax.slice_in_dim(block, block.shape[dim] - width, None, axis=dim), axis, forward
        )
        high = lax.ppermute(lax.slice_in_dim(block, 0, width, axis=dim), axis, backward)
        block = jnp.concatenate([low, block, high], axis=dim)
    return block


def table(values):
    return jnp.asarray(values, dtype=jnp.float32)


def pole_values(deviation):
    normal_sum = 0.0
    for cos_weight, sin_weight, decay, freq in DERICHE_POLES:
        magnitude = math.exp(-decay / deviation)
        real_z = magnitude * math.cos(freq / deviation)
        imag_z = magnitude * math.sin(freq / deviation)
        denom = (1.0 - real_z) ** 2 + imag_z**2
        real_q = (real_z - magnitude * magnitude) / denom
        imag_q = imag_z / denom
        normal_sum += cos_weight + 2.0 * (cos_weight * real_q + sin_weight * imag_q)
    pole_list = []
    for cos_weight, sin_weight, decay, freq in DERICHE_POLES:
        pole_list.append(
            (cos_weight / normal_sum, -sin_weight / normal_sum, decay / deviation, freq / deviation)
        )
    return pole_list


def pole_power(rate, freq, counts):
    magnitude = np.exp(-rate * counts)
    return (magnitude * np.cos(freq * counts), magnitude * np.sin(freq * counts))


def filter_tables(length, deviation):
    positions = np.arange(length) + 0.0
    distance = np.abs(positions[:, None] - positions[None, :])
    kernel = np.zeros((length, length))
    summary = np.zeros((2, 2, 2, length))
    inject = np.zeros((2, 2, 2, length))
    stride_power = np.zeros((2, 2))
    for index, (real_a, imag_a, rate, freq) in enumerate(pole_values(deviation)):
        dist_re, dist_im = pole_power(rate, freq, distance)
        kernel += real_a * dist_re - imag_a * dist_im
        back_re, back_im = pole_power(rate, freq, length - 1 - positions)
        summary[0, 0, index] = back_re
        summary[0, 1, index] = back_im
        fwd_re, fwd_im = pole_power(rate, freq, positions)
        summary[1, 0, index] = fwd_re
        summary[1, 1, index] = fwd_im
        next_re, next_im = pole_power(rate, freq, positions + 1)
        inject[0, 0, index] = real_a * next_re - imag_a * next_im
        inject[0, 1, index] = -(real_a * next_im + imag_a * next_re)
        rest_re, rest_im = pole_power(rate, freq, length - positions)
        inject[1, 0, index] = real_a * rest_re - imag_a * rest_im
        inject[1, 1, index] = -(real_a * rest_im + imag_a * rest_re)
        whole_re, whole_im = pole_power(rate, freq, length + 0.0)
        stride_power[0, index] = whole_re
        stride_power[1, index] = whole_im
    return (kernel, summary, inject, stride_power)


def tap_sum(source, coeffs, axis, length):
    accum = coeffs[0] * lax.slice_in_dim(source, 0, length, axis=axis)
    for offset in range(1, 9):
        accum = accum + coeffs[offset] * lax.slice_in_dim(
            source, offset, offset + length, axis=axis
        )
    return accum


def derivative_fields(padded, rows, cols):
    along_cols = tap_sum(padded, DER_FIRST, 1, cols)
    center = padded[4 : 4 + rows, 4 : 4 + cols]
    grad_x = along_cols[4 : 4 + rows]
    grad_y = tap_sum(padded[:, 4 : 4 + cols], DER_FIRST, 0, rows)
    curve_xx = tap_sum(padded[4 : 4 + rows], DER_SECOND, 1, cols)
    curve_xy = tap_sum(along_cols, DER_FIRST, 0, rows)
    curve_yy = tap_sum(padded[:, 4 : 4 + cols], DER_SECOND, 0, rows)
    return jnp.stack([center, grad_x, grad_y, curve_xx, curve_xy, curve_yy])


def complex_mul(left, right):
    real_part = left[0] * right[0] - left[1] * right[1]
    imag_part = left[0] * right[1] + left[1] * right[0]
    return jnp.stack([real_part, imag_part])


def chain_carry(local_sum, stride_power, count, mover):

    def advance(index, state):
        return mover(complex_mul(stride_power, state) + local_sum)

    return lax.fori_loop(0, count - 1, advance, jnp.zeros_like(local_sum))


def col_carries(forward, backward, stride_power):
    count = lax.axis_size("col")
    left_in = chain_carry(
        forward, stride_power, count, lambda payload: passed_along(payload, "col", 1)
    )
    right_in = chain_carry(
        backward, stride_power, count, lambda payload: passed_along(payload, "col", -1)
    )
    return (left_in, right_in)


def row_carries(forward, backward, stride_power):
    count = lax.axis_size("row")
    upper_in = chain_carry(
        forward, stride_power, count, lambda payload: passed_along(payload, "row", 1)
    )
    lower_in = chain_carry(
        backward, stride_power, count, lambda payload: passed_along(payload, "row", -1)
    )
    return (upper_in, lower_in)


def on_device(image):
    rows_dev, cols_dev = image.shape
    padded = extended(image, (("row", 0), ("col", 1)), 4)
    fields = derivative_fields(padded, rows_dev, cols_dev)
    deviations = (SIG_A, SIG_B)
    col_tables = [filter_tables(cols_dev, deviation) for deviation in deviations]
    row_tables = [filter_tables(rows_dev, deviation) for deviation in deviations]
    flat_rows = fields.reshape(6 * rows_dev, cols_dev)
    col_summary = np.concatenate([tables[1][:, :, None] for tables in col_tables], axis=2).reshape(
        16, cols_dev
    )
    col_power = np.concatenate([tables[3] for tables in col_tables], axis=1)[:, :, None]
    col_sums = jnp.einsum("kc,fc->kf", table(col_summary), flat_rows, precision=HIGHEST).reshape(
        2, 2, 4, 6 * rows_dev
    )
    left_in, right_in = col_carries(col_sums[0], col_sums[1], table(col_power))
    smoothed = []
    for level in range(2):
        kernel, summary, inject, stride_power = col_tables[level]
        blended = jnp.dot(flat_rows, table(kernel), precision=HIGHEST)
        blended = blended + jnp.einsum(
            "rpf,rpj->fj",
            left_in[:, 2 * level : 2 * level + 2],
            table(inject[0]),
            precision=HIGHEST,
        )
        blended = blended + jnp.einsum(
            "rpf,rpj->fj",
            right_in[:, 2 * level : 2 * level + 2],
            table(inject[1]),
            precision=HIGHEST,
        )
        smoothed.append(blended.reshape(6, rows_dev, cols_dev))
    row_sums = []
    for level in range(2):
        summary = row_tables[level][1].reshape(8, rows_dev)
        partial_sums = jnp.einsum("kj,fjc->kfc", table(summary), smoothed[level], precision=HIGHEST)
        row_sums.append(partial_sums.reshape(2, 2, 2, 6 * cols_dev))
    row_sums = jnp.concatenate(row_sums, axis=2)
    row_power = np.concatenate([tables[3] for tables in row_tables], axis=1)[:, :, None]
    upper_in, lower_in = row_carries(row_sums[0], row_sums[1], table(row_power))
    results = []
    for level in range(2):
        kernel, summary, inject, stride_power = row_tables[level]
        deviation = deviations[level]
        blended = jnp.einsum("ij,fjc->fic", table(kernel), smoothed[level], precision=HIGHEST)
        upper_part = upper_in[:, 2 * level : 2 * level + 2].reshape(2, 2, 6, cols_dev)
        lower_part = lower_in[:, 2 * level : 2 * level + 2].reshape(2, 2, 6, cols_dev)
        blended = blended + jnp.einsum(
            "rpfc,rpi->fic", upper_part, table(inject[0]), precision=HIGHEST
        )
        blended = blended + jnp.einsum(
            "rpfc,rpi->fic", lower_part, table(inject[1]), precision=HIGHEST
        )
        base = 2.0 * math.sqrt(math.pi) * deviation
        factors = jnp.array(
            [
                base,
                base * deviation,
                base * deviation,
                base * deviation**2,
                base * deviation**2,
                base * deviation**2,
            ],
            jnp.float32,
        )
        results.append(blended * factors[:, None, None])
    return jnp.concatenate(results, axis=0).astype(jnp.bfloat16)


def solution(mesh):
    placed = (P("row", "col"),)
    return jax.shard_map(
        on_device, mesh=mesh, in_specs=placed, out_specs=P(None, "row", "col"), check_vma=False
    )
```

profile of v0, /device:TPU:121, one launch (start us, length us, event | category | flops | bytes accessed | tf_op | source)
XLA Modules:
  0.0 502.6 jit_solution(8723181667054544776)
XLA Ops:
  26.4 98.3 %while.44 = (s32[]{:T(128)}, f32[2,4,768]{2,1,0:T(4,128)S(1)}, f32[2,4,768]{2,1,0:T(4,128)S(1)}, s32[]{:T(128)}, f32[4]{0:T(128)S(1)}, /*index=5*/f32[4]{0:T(128)S(1)}) while((s32[]{:T(128)}, f32[2,4,768]{2,1,0:T(4,128)S(1)}, f32[2,4,768]{2,1,0:T(4,128)S(1)}, s32[]{:T(128)}, f32[4]{0:T(128)S(1)}, ...), condition=%wide.region_1.0_spmd.clone, body=%wide.region_0.0_spmd.sunk.clone.sunk | while | flops 30722 | bytes 221325 | solution.py:144
  36.5 5.7 %collective-permute-start = (f32[2,4,768]{2,1,0:T(4,128)S(1)}, f32[2,4,768]{2,1,0:T(4,128)S(1)}, u32[]{:S(2)}, u32[]{:S(2)}) collective-permute-start(f32[2,4,768]{2,1,0:T(4,128)S(1)} %maximum_add_fusion.8), channel_id=1, source_target_pairs={{0,1},{1,2},{2,3},{3,4},{4,5},{5,6},{6,7},{7,8},{8,9},{9,10},{10,1... | collective-permute-start | bytes 73736 | tf_op jit(solution)/shard_map/while/body/eval_jaxpr/ppermute | solution.py:42
  43.3 5.7 %collective-permute-start = (f32[2,4,768]{2,1,0:T(4,128)S(1)}, f32[2,4,768]{2,1,0:T(4,128)S(1)}, u32[]{:S(2)}, u32[]{:S(2)}) collective-permute-start(f32[2,4,768]{2,1,0:T(4,128)S(1)} %maximum_add_fusion.8), channel_id=1, source_target_pairs={{0,1},{1,2},{2,3},{3,4},{4,5},{5,6},{6,7},{7,8},{8,9},{9,10},{10,1... | collective-permute-start | bytes 73736 | tf_op jit(solution)/shard_map/while/body/eval_jaxpr/ppermute | solution.py:42
  50.0 5.7 %collective-permute-start = (f32[2,4,768]{2,1,0:T(4,128)S(1)}, f32[2,4,768]{2,1,0:T(4,128)S(1)}, u32[]{:S(2)}, u32[]{:S(2)}) collective-permute-start(f32[2,4,768]{2,1,0:T(4,128)S(1)} %maximum_add_fusion.8), channel_id=1, source_target_pairs={{0,1},{1,2},{2,3},{3,4},{4,5},{5,6},{6,7},{7,8},{8,9},{9,10},{10,1... | collective-permute-start | bytes 73736 | tf_op jit(solution)/shard_map/while/body/eval_jaxpr/ppermute | solution.py:42
  56.8 5.7 %collective-permute-start = (f32[2,4,768]{2,1,0:T(4,128)S(1)}, f32[2,4,768]{2,1,0:T(4,128)S(1)}, u32[]{:S(2)}, u32[]{:S(2)}) collective-permute-start(f32[2,4,768]{2,1,0:T(4,128)S(1)} %maximum_add_fusion.8), channel_id=1, source_target_pairs={{0,1},{1,2},{2,3},{3,4},{4,5},{5,6},{6,7},{7,8},{8,9},{9,10},{10,1... | collective-permute-start | bytes 73736 | tf_op jit(solution)/shard_map/while/body/eval_jaxpr/ppermute | solution.py:42
  63.6 5.7 %collective-permute-start = (f32[2,4,768]{2,1,0:T(4,128)S(1)}, f32[2,4,768]{2,1,0:T(4,128)S(1)}, u32[]{:S(2)}, u32[]{:S(2)}) collective-permute-start(f32[2,4,768]{2,1,0:T(4,128)S(1)} %maximum_add_fusion.8), channel_id=1, source_target_pairs={{0,1},{1,2},{2,3},{3,4},{4,5},{5,6},{6,7},{7,8},{8,9},{9,10},{10,1... | collective-permute-start | bytes 73736 | tf_op jit(solution)/shard_map/while/body/eval_jaxpr/ppermute | solution.py:42
  70.3 5.7 %collective-permute-start = (f32[2,4,768]{2,1,0:T(4,128)S(1)}, f32[2,4,768]{2,1,0:T(4,128)S(1)}, u32[]{:S(2)}, u32[]{:S(2)}) collective-permute-start(f32[2,4,768]{2,1,0:T(4,128)S(1)} %maximum_add_fusion.8), channel_id=1, source_target_pairs={{0,1},{1,2},{2,3},{3,4},{4,5},{5,6},{6,7},{7,8},{8,9},{9,10},{10,1... | collective-permute-start | bytes 73736 | tf_op jit(solution)/shard_map/while/body/eval_jaxpr/ppermute | solution.py:42
  77.1 6.0 %collective-permute-start = (f32[2,4,768]{2,1,0:T(4,128)S(1)}, f32[2,4,768]{2,1,0:T(4,128)S(1)}, u32[]{:S(2)}, u32[]{:S(2)}) collective-permute-start(f32[2,4,768]{2,1,0:T(4,128)S(1)} %maximum_add_fusion.8), channel_id=1, source_target_pairs={{0,1},{1,2},{2,3},{3,4},{4,5},{5,6},{6,7},{7,8},{8,9},{9,10},{10,1... | collective-permute-start | bytes 73736 | tf_op jit(solution)/shard_map/while/body/eval_jaxpr/ppermute | solution.py:42
  84.1 5.7 %collective-permute-start = (f32[2,4,768]{2,1,0:T(4,128)S(1)}, f32[2,4,768]{2,1,0:T(4,128)S(1)}, u32[]{:S(2)}, u32[]{:S(2)}) collective-permute-start(f32[2,4,768]{2,1,0:T(4,128)S(1)} %maximum_add_fusion.8), channel_id=1, source_target_pairs={{0,1},{1,2},{2,3},{3,4},{4,5},{5,6},{6,7},{7,8},{8,9},{9,10},{10,1... | collective-permute-start | bytes 73736 | tf_op jit(solution)/shard_map/while/body/eval_jaxpr/ppermute | solution.py:42
  90.9 5.7 %collective-permute-start = (f32[2,4,768]{2,1,0:T(4,128)S(1)}, f32[2,4,768]{2,1,0:T(4,128)S(1)}, u32[]{:S(2)}, u32[]{:S(2)}) collective-permute-start(f32[2,4,768]{2,1,0:T(4,128)S(1)} %maximum_add_fusion.8), channel_id=1, source_target_pairs={{0,1},{1,2},{2,3},{3,4},{4,5},{5,6},{6,7},{7,8},{8,9},{9,10},{10,1... | collective-permute-start | bytes 73736 | tf_op jit(solution)/shard_map/while/body/eval_jaxpr/ppermute | solution.py:42
  97.6 5.7 %collective-permute-start = (f32[2,4,768]{2,1,0:T(4,128)S(1)}, f32[2,4,768]{2,1,0:T(4,128)S(1)}, u32[]{:S(2)}, u32[]{:S(2)}) collective-permute-start(f32[2,4,768]{2,1,0:T(4,128)S(1)} %maximum_add_fusion.8), channel_id=1, source_target_pairs={{0,1},{1,2},{2,3},{3,4},{4,5},{5,6},{6,7},{7,8},{8,9},{9,10},{10,1... | collective-permute-start | bytes 73736 | tf_op jit(solution)/shard_map/while/body/eval_jaxpr/ppermute | solution.py:42
  104.4 5.7 %collective-permute-start = (f32[2,4,768]{2,1,0:T(4,128)S(1)}, f32[2,4,768]{2,1,0:T(4,128)S(1)}, u32[]{:S(2)}, u32[]{:S(2)}) collective-permute-start(f32[2,4,768]{2,1,0:T(4,128)S(1)} %maximum_add_fusion.8), channel_id=1, source_target_pairs={{0,1},{1,2},{2,3},{3,4},{4,5},{5,6},{6,7},{7,8},{8,9},{9,10},{10,1... | collective-permute-start | bytes 73736 | tf_op jit(solution)/shard_map/while/body/eval_jaxpr/ppermute | solution.py:42
  111.2 5.7 %collective-permute-start = (f32[2,4,768]{2,1,0:T(4,128)S(1)}, f32[2,4,768]{2,1,0:T(4,128)S(1)}, u32[]{:S(2)}, u32[]{:S(2)}) collective-permute-start(f32[2,4,768]{2,1,0:T(4,128)S(1)} %maximum_add_fusion.8), channel_id=1, source_target_pairs={{0,1},{1,2},{2,3},{3,4},{4,5},{5,6},{6,7},{7,8},{8,9},{9,10},{10,1... | collective-permute-start | bytes 73736 | tf_op jit(solution)/shard_map/while/body/eval_jaxpr/ppermute | solution.py:42
  126.1 102.1 %while.45 = (s32[]{:T(128)}, f32[2,4,768]{2,1,0:T(4,128)S(1)}, f32[2,4,768]{2,1,0:T(4,128)S(1)}, s32[]{:T(128)}, f32[4]{0:T(128)S(1)}, /*index=5*/f32[4]{0:T(128)S(1)}) while((s32[]{:T(128)}, f32[2,4,768]{2,1,0:T(4,128)S(1)}, f32[2,4,768]{2,1,0:T(4,128)S(1)}, s32[]{:T(128)}, f32[4]{0:T(128)S(1)}, ...), condition=%wide.region_3.0_spmd.clone, body=%wide.region_2.0_spmd.sunk.clone.sunk | while | flops 30722 | bytes 221325 | solution.py:144
  234.1 145.9 %while.46 = (s32[]{:T(128)}, f32[2,4,768]{2,1,0:T(4,128)S(1)}, f32[2,4,768]{2,1,0:T(4,128)S(1)}, s32[]{:T(128)}, f32[4]{0:T(128)S(1)}, /*index=5*/f32[4]{0:T(128)S(1)}) while((s32[]{:T(128)}, f32[2,4,768]{2,1,0:T(4,128)S(1)}, f32[2,4,768]{2,1,0:T(4,128)S(1)}, s32[]{:T(128)}, f32[4]{0:T(128)S(1)}, ...), condition=%wide.region_5.0_spmd.clone, body=%wide.region_4.0_spmd.sunk.clone.sunk | while | flops 30722 | bytes 221325 | solution.py:144
  234.2 38.0 %collective-permute-start.2 = (f32[2,4,768]{2,1,0:T(4,128)S(1)}, f32[2,4,768]{2,1,0:T(4,128)S(1)}, u32[]{:S(2)}, u32[]{:S(2)}) collective-permute-start(f32[2,4,768]{2,1,0:T(4,128)S(1)} %maximum_add_fusion.10), channel_id=1, source_target_pairs={{0,16},{16,32},{32,48},{48,64},{64,80},{80,96},{96,112},{112,128},... | collective-permute-start | bytes 73736 | tf_op jit(solution)/shard_map/while/body/eval_jaxpr/ppermute | solution.py:42
  273.2 6.6 %collective-permute-start.2 = (f32[2,4,768]{2,1,0:T(4,128)S(1)}, f32[2,4,768]{2,1,0:T(4,128)S(1)}, u32[]{:S(2)}, u32[]{:S(2)}) collective-permute-start(f32[2,4,768]{2,1,0:T(4,128)S(1)} %maximum_add_fusion.10), channel_id=1, source_target_pairs={{0,16},{16,32},{32,48},{48,64},{64,80},{80,96},{96,112},{112,128},... | collective-permute-start | bytes 73736 | tf_op jit(solution)/shard_map/while/body/eval_jaxpr/ppermute | solution.py:42
  280.9 6.6 %collective-permute-start.2 = (f32[2,4,768]{2,1,0:T(4,128)S(1)}, f32[2,4,768]{2,1,0:T(4,128)S(1)}, u32[]{:S(2)}, u32[]{:S(2)}) collective-permute-start(f32[2,4,768]{2,1,0:T(4,128)S(1)} %maximum_add_fusion.10), channel_id=1, source_target_pairs={{0,16},{16,32},{32,48},{48,64},{64,80},{80,96},{96,112},{112,128},... | collective-permute-start | bytes 73736 | tf_op jit(solution)/shard_map/while/body/eval_jaxpr/ppermute | solution.py:42
  288.5 6.6 %collective-permute-start.2 = (f32[2,4,768]{2,1,0:T(4,128)S(1)}, f32[2,4,768]{2,1,0:T(4,128)S(1)}, u32[]{:S(2)}, u32[]{:S(2)}) collective-permute-start(f32[2,4,768]{2,1,0:T(4,128)S(1)} %maximum_add_fusion.10), channel_id=1, source_target_pairs={{0,16},{16,32},{32,48},{48,64},{64,80},{80,96},{96,112},{112,128},... | collective-permute-start | bytes 73736 | tf_op jit(solution)/shard_map/while/body/eval_jaxpr/ppermute | solution.py:42
  296.1 6.6 %collective-permute-start.2 = (f32[2,4,768]{2,1,0:T(4,128)S(1)}, f32[2,4,768]{2,1,0:T(4,128)S(1)}, u32[]{:S(2)}, u32[]{:S(2)}) collective-permute-start(f32[2,4,768]{2,1,0:T(4,128)S(1)} %maximum_add_fusion.10), channel_id=1, source_target_pairs={{0,16},{16,32},{32,48},{48,64},{64,80},{80,96},{96,112},{112,128},... | collective-permute-start | bytes 73736 | tf_op jit(solution)/shard_map/while/body/eval_jaxpr/ppermute | solution.py:42
  303.8 6.6 %collective-permute-start.2 = (f32[2,4,768]{2,1,0:T(4,128)S(1)}, f32[2,4,768]{2,1,0:T(4,128)S(1)}, u32[]{:S(2)}, u32[]{:S(2)}) collective-permute-start(f32[2,4,768]{2,1,0:T(4,128)S(1)} %maximum_add_fusion.10), channel_id=1, source_target_pairs={{0,16},{16,32},{32,48},{48,64},{64,80},{80,96},{96,112},{112,128},... | collective-permute-start | bytes 73736 | tf_op jit(solution)/shard_map/while/body/eval_jaxpr/ppermute | solution.py:42
  311.4 6.6 %collective-permute-start.2 = (f32[2,4,768]{2,1,0:T(4,128)S(1)}, f32[2,4,768]{2,1,0:T(4,128)S(1)}, u32[]{:S(2)}, u32[]{:S(2)}) collective-permute-start(f32[2,4,768]{2,1,0:T(4,128)S(1)} %maximum_add_fusion.10), channel_id=1, source_target_pairs={{0,16},{16,32},{32,48},{48,64},{64,80},{80,96},{96,112},{112,128},... | collective-permute-start | bytes 73736 | tf_op jit(solution)/shard_map/while/body/eval_jaxpr/ppermute | solution.py:42
  319.0 6.6 %collective-permute-start.2 = (f32[2,4,768]{2,1,0:T(4,128)S(1)}, f32[2,4,768]{2,1,0:T(4,128)S(1)}, u32[]{:S(2)}, u32[]{:S(2)}) collective-permute-start(f32[2,4,768]{2,1,0:T(4,128)S(1)} %maximum_add_fusion.10), channel_id=1, source_target_pairs={{0,16},{16,32},{32,48},{48,64},{64,80},{80,96},{96,112},{112,128},... | collective-permute-start | bytes 73736 | tf_op jit(solution)/shard_map/while/body/eval_jaxpr/ppermute | solution.py:42
  326.7 6.6 %collective-permute-start.2 = (f32[2,4,768]{2,1,0:T(4,128)S(1)}, f32[2,4,768]{2,1,0:T(4,128)S(1)}, u32[]{:S(2)}, u32[]{:S(2)}) collective-permute-start(f32[2,4,768]{2,1,0:T(4,128)S(1)} %maximum_add_fusion.10), channel_id=1, source_target_pairs={{0,16},{16,32},{32,48},{48,64},{64,80},{80,96},{96,112},{112,128},... | collective-permute-start | bytes 73736 | tf_op jit(solution)/shard_map/while/body/eval_jaxpr/ppermute | solution.py:42
  334.3 6.6 %collective-permute-start.2 = (f32[2,4,768]{2,1,0:T(4,128)S(1)}, f32[2,4,768]{2,1,0:T(4,128)S(1)}, u32[]{:S(2)}, u32[]{:S(2)}) collective-permute-start(f32[2,4,768]{2,1,0:T(4,128)S(1)} %maximum_add_fusion.10), channel_id=1, source_target_pairs={{0,16},{16,32},{32,48},{48,64},{64,80},{80,96},{96,112},{112,128},... | collective-permute-start | bytes 73736 | tf_op jit(solution)/shard_map/while/body/eval_jaxpr/ppermute | solution.py:42
  342.0 6.6 %collective-permute-start.2 = (f32[2,4,768]{2,1,0:T(4,128)S(1)}, f32[2,4,768]{2,1,0:T(4,128)S(1)}, u32[]{:S(2)}, u32[]{:S(2)}) collective-permute-start(f32[2,4,768]{2,1,0:T(4,128)S(1)} %maximum_add_fusion.10), channel_id=1, source_target_pairs={{0,16},{16,32},{32,48},{48,64},{64,80},{80,96},{96,112},{112,128},... | collective-permute-start | bytes 73736 | tf_op jit(solution)/shard_map/while/body/eval_jaxpr/ppermute | solution.py:42
  349.6 6.6 %collective-permute-start.2 = (f32[2,4,768]{2,1,0:T(4,128)S(1)}, f32[2,4,768]{2,1,0:T(4,128)S(1)}, u32[]{:S(2)}, u32[]{:S(2)}) collective-permute-start(f32[2,4,768]{2,1,0:T(4,128)S(1)} %maximum_add_fusion.10), channel_id=1, source_target_pairs={{0,16},{16,32},{32,48},{48,64},{64,80},{80,96},{96,112},{112,128},... | collective-permute-start | bytes 73736 | tf_op jit(solution)/shard_map/while/body/eval_jaxpr/ppermute | solution.py:42
  357.2 6.6 %collective-permute-start.2 = (f32[2,4,768]{2,1,0:T(4,128)S(1)}, f32[2,4,768]{2,1,0:T(4,128)S(1)}, u32[]{:S(2)}, u32[]{:S(2)}) collective-permute-start(f32[2,4,768]{2,1,0:T(4,128)S(1)} %maximum_add_fusion.10), channel_id=1, source_target_pairs={{0,16},{16,32},{32,48},{48,64},{64,80},{80,96},{96,112},{112,128},... | collective-permute-start | bytes 73736 | tf_op jit(solution)/shard_map/while/body/eval_jaxpr/ppermute | solution.py:42
  364.9 6.6 %collective-permute-start.2 = (f32[2,4,768]{2,1,0:T(4,128)S(1)}, f32[2,4,768]{2,1,0:T(4,128)S(1)}, u32[]{:S(2)}, u32[]{:S(2)}) collective-permute-start(f32[2,4,768]{2,1,0:T(4,128)S(1)} %maximum_add_fusion.10), channel_id=1, source_target_pairs={{0,16},{16,32},{32,48},{48,64},{64,80},{80,96},{96,112},{112,128},... | collective-permute-start | bytes 73736 | tf_op jit(solution)/shard_map/while/body/eval_jaxpr/ppermute | solution.py:42
  372.5 6.6 %collective-permute-start.2 = (f32[2,4,768]{2,1,0:T(4,128)S(1)}, f32[2,4,768]{2,1,0:T(4,128)S(1)}, u32[]{:S(2)}, u32[]{:S(2)}) collective-permute-start(f32[2,4,768]{2,1,0:T(4,128)S(1)} %maximum_add_fusion.10), channel_id=1, source_target_pairs={{0,16},{16,32},{32,48},{48,64},{64,80},{80,96},{96,112},{112,128},... | collective-permute-start | bytes 73736 | tf_op jit(solution)/shard_map/while/body/eval_jaxpr/ppermute | solution.py:42
  380.8 115.2 %while.47 = (s32[]{:T(128)}, f32[2,4,768]{2,1,0:T(4,128)S(1)}, f32[2,4,768]{2,1,0:T(4,128)S(1)}, s32[]{:T(128)}, f32[4]{0:T(128)S(1)}, /*index=5*/f32[4]{0:T(128)S(1)}) while((s32[]{:T(128)}, f32[2,4,768]{2,1,0:T(4,128)S(1)}, f32[2,4,768]{2,1,0:T(4,128)S(1)}, s32[]{:T(128)}, f32[4]{0:T(128)S(1)}, ...), condition=%wide.region_7.0_spmd.clone, body=%wide.region_6.0_spmd.sunk.clone.sunk | while | flops 30722 | bytes 221325 | solution.py:144
  382.8 6.2 %collective-permute-done.3 = f32[2,4,768]{2,1,0:T(4,128)S(1)} collective-permute-done((f32[2,4,768]{2,1,0:T(4,128)S(1)}, f32[2,4,768]{2,1,0:T(4,128)S(1)}, u32[]{:S(2)}, u32[]{:S(2)}) %collective-permute-start.3) | collective-permute-done | bytes 24608 | tf_op jit(solution)/shard_map/while/body/eval_jaxpr/ppermute | solution.py:42
  (320 shorter events, 295.2 us)
Async XLA Ops:
  0.7 7.3 %collective-permute-start.4 = (f32[4,128]{1,0:T(4,128)S(1)}, f32[4,128]{1,0:T(4,128)S(1)}, u32[]{:S(2)}, u32[]{:S(2)}) collective-permute-start(f32[4,128]{1,0:T(4,128)S(1)} %get-tuple-element.181), channel_id=1, source_target_pairs={{0,16},{16,32},{32,48},{48,64},{64,80},{80,96},{96,112},{112,128},... | collective-permute-start | bytes 6152 | tf_op jit(solution)/shard_map/ppermute | solution.py:50
  5.1 7.4 %collective-permute-start.5 = (f32[4,128]{1,0:T(4,128)S(1)}, f32[4,128]{1,0:T(4,128)S(1)}, u32[]{:S(2)}, u32[]{:S(2)}) collective-permute-start(f32[4,128]{1,0:T(4,128)S(1)} %get-tuple-element.182), channel_id=1, source_target_pairs={{16,0},{32,16},{48,32},{64,48},{80,64},{96,80},{112,96},{128,112},... | collective-permute-start | bytes 6152 | tf_op jit(solution)/shard_map/ppermute | solution.py:53
  234.2 38.9 %collective-permute-start.2 = (f32[2,4,768]{2,1,0:T(4,128)S(1)}, f32[2,4,768]{2,1,0:T(4,128)S(1)}, u32[]{:S(2)}, u32[]{:S(2)}) collective-permute-start(f32[2,4,768]{2,1,0:T(4,128)S(1)} %maximum_add_fusion.10), channel_id=1, source_target_pairs={{0,16},{16,32},{32,48},{48,64},{64,80},{80,96},{96,112},{112,128},... | collective-permute-start | bytes 73736 | tf_op jit(solution)/shard_map/while/body/eval_jaxpr/ppermute | solution.py:42
  273.2 7.5 %collective-permute-start.2 = (f32[2,4,768]{2,1,0:T(4,128)S(1)}, f32[2,4,768]{2,1,0:T(4,128)S(1)}, u32[]{:S(2)}, u32[]{:S(2)}) collective-permute-start(f32[2,4,768]{2,1,0:T(4,128)S(1)} %maximum_add_fusion.10), channel_id=1, source_target_pairs={{0,16},{16,32},{32,48},{48,64},{64,80},{80,96},{96,112},{112,128},... | collective-permute-start | bytes 73736 | tf_op jit(solution)/shard_map/while/body/eval_jaxpr/ppermute | solution.py:42
  280.9 7.5 %collective-permute-start.2 = (f32[2,4,768]{2,1,0:T(4,128)S(1)}, f32[2,4,768]{2,1,0:T(4,128)S(1)}, u32[]{:S(2)}, u32[]{:S(2)}) collective-permute-start(f32[2,4,768]{2,1,0:T(4,128)S(1)} %maximum_add_fusion.10), channel_id=1, source_target_pairs={{0,16},{16,32},{32,48},{48,64},{64,80},{80,96},{96,112},{112,128},... | collective-permute-start | bytes 73736 | tf_op jit(solution)/shard_map/while/body/eval_jaxpr/ppermute | solution.py:42
  288.5 7.5 %collective-permute-start.2 = (f32[2,4,768]{2,1,0:T(4,128)S(1)}, f32[2,4,768]{2,1,0:T(4,128)S(1)}, u32[]{:S(2)}, u32[]{:S(2)}) collective-permute-start(f32[2,4,768]{2,1,0:T(4,128)S(1)} %maximum_add_fusion.10), channel_id=1, source_target_pairs={{0,16},{16,32},{32,48},{48,64},{64,80},{80,96},{96,112},{112,128},... | collective-permute-start | bytes 73736 | tf_op jit(solution)/shard_map/while/body/eval_jaxpr/ppermute | solution.py:42
  296.1 7.5 %collective-permute-start.2 = (f32[2,4,768]{2,1,0:T(4,128)S(1)}, f32[2,4,768]{2,1,0:T(4,128)S(1)}, u32[]{:S(2)}, u32[]{:S(2)}) collective-permute-start(f32[2,4,768]{2,1,0:T(4,128)S(1)} %maximum_add_fusion.10), channel_id=1, source_target_pairs={{0,16},{16,32},{32,48},{48,64},{64,80},{80,96},{96,112},{112,128},... | collective-permute-start | bytes 73736 | tf_op jit(solution)/shard_map/while/body/eval_jaxpr/ppermute | solution.py:42
  303.8 7.5 %collective-permute-start.2 = (f32[2,4,768]{2,1,0:T(4,128)S(1)}, f32[2,4,768]{2,1,0:T(4,128)S(1)}, u32[]{:S(2)}, u32[]{:S(2)}) collective-permute-start(f32[2,4,768]{2,1,0:T(4,128)S(1)} %maximum_add_fusion.10), channel_id=1, source_target_pairs={{0,16},{16,32},{32,48},{48,64},{64,80},{80,96},{96,112},{112,128},... | collective-permute-start | bytes 73736 | tf_op jit(solution)/shard_map/while/body/eval_jaxpr/ppermute | solution.py:42
  311.4 7.5 %collective-permute-start.2 = (f32[2,4,768]{2,1,0:T(4,128)S(1)}, f32[2,4,768]{2,1,0:T(4,128)S(1)}, u32[]{:S(2)}, u32[]{:S(2)}) collective-permute-start(f32[2,4,768]{2,1,0:T(4,128)S(1)} %maximum_add_fusion.10), channel_id=1, source_target_pairs={{0,16},{16,32},{32,48},{48,64},{64,80},{80,96},{96,112},{112,128},... | collective-permute-start | bytes 73736 | tf_op jit(solution)/shard_map/while/body/eval_jaxpr/ppermute | solution.py:42
  319.0 7.5 %collective-permute-start.2 = (f32[2,4,768]{2,1,0:T(4,128)S(1)}, f32[2,4,768]{2,1,0:T(4,128)S(1)}, u32[]{:S(2)}, u32[]{:S(2)}) collective-permute-start(f32[2,4,768]{2,1,0:T(4,128)S(1)} %maximum_add_fusion.10), channel_id=1, source_target_pairs={{0,16},{16,32},{32,48},{48,64},{64,80},{80,96},{96,112},{112,128},... | collective-permute-start | bytes 73736 | tf_op jit(solution)/shard_map/while/body/eval_jaxpr/ppermute | solution.py:42
  326.7 7.5 %collective-permute-start.2 = (f32[2,4,768]{2,1,0:T(4,128)S(1)}, f32[2,4,768]{2,1,0:T(4,128)S(1)}, u32[]{:S(2)}, u32[]{:S(2)}) collective-permute-start(f32[2,4,768]{2,1,0:T(4,128)S(1)} %maximum_add_fusion.10), channel_id=1, source_target_pairs={{0,16},{16,32},{32,48},{48,64},{64,80},{80,96},{96,112},{112,128},... | collective-permute-start | bytes 73736 | tf_op jit(solution)/shard_map/while/body/eval_jaxpr/ppermute | solution.py:42
  334.3 7.5 %collective-permute-start.2 = (f32[2,4,768]{2,1,0:T(4,128)S(1)}, f32[2,4,768]{2,1,0:T(4,128)S(1)}, u32[]{:S(2)}, u32[]{:S(2)}) collective-permute-start(f32[2,4,768]{2,1,0:T(4,128)S(1)} %maximum_add_fusion.10), channel_id=1, source_target_pairs={{0,16},{16,32},{32,48},{48,64},{64,80},{80,96},{96,112},{112,128},... | collective-permute-start | bytes 73736 | tf_op jit(solution)/shard_map/while/body/eval_jaxpr/ppermute | solution.py:42
  342.0 7.5 %collective-permute-start.2 = (f32[2,4,768]{2,1,0:T(4,128)S(1)}, f32[2,4,768]{2,1,0:T(4,128)S(1)}, u32[]{:S(2)}, u32[]{:S(2)}) collective-permute-start(f32[2,4,768]{2,1,0:T(4,128)S(1)} %maximum_add_fusion.10), channel_id=1, source_target_pairs={{0,16},{16,32},{32,48},{48,64},{64,80},{80,96},{96,112},{112,128},... | collective-permute-start | bytes 73736 | tf_op jit(solution)/shard_map/while/body/eval_jaxpr/ppermute | solution.py:42
  349.6 7.5 %collective-permute-start.2 = (f32[2,4,768]{2,1,0:T(4,128)S(1)}, f32[2,4,768]{2,1,0:T(4,128)S(1)}, u32[]{:S(2)}, u32[]{:S(2)}) collective-permute-start(f32[2,4,768]{2,1,0:T(4,128)S(1)} %maximum_add_fusion.10), channel_id=1, source_target_pairs={{0,16},{16,32},{32,48},{48,64},{64,80},{80,96},{96,112},{112,128},... | collective-permute-start | bytes 73736 | tf_op jit(solution)/shard_map/while/body/eval_jaxpr/ppermute | solution.py:42
  357.2 7.5 %collective-permute-start.2 = (f32[2,4,768]{2,1,0:T(4,128)S(1)}, f32[2,4,768]{2,1,0:T(4,128)S(1)}, u32[]{:S(2)}, u32[]{:S(2)}) collective-permute-start(f32[2,4,768]{2,1,0:T(4,128)S(1)} %maximum_add_fusion.10), channel_id=1, source_target_pairs={{0,16},{16,32},{32,48},{48,64},{64,80},{80,96},{96,112},{112,128},... | collective-permute-start | bytes 73736 | tf_op jit(solution)/shard_map/while/body/eval_jaxpr/ppermute | solution.py:42
  364.9 7.5 %collective-permute-start.2 = (f32[2,4,768]{2,1,0:T(4,128)S(1)}, f32[2,4,768]{2,1,0:T(4,128)S(1)}, u32[]{:S(2)}, u32[]{:S(2)}) collective-permute-start(f32[2,4,768]{2,1,0:T(4,128)S(1)} %maximum_add_fusion.10), channel_id=1, source_target_pairs={{0,16},{16,32},{32,48},{48,64},{64,80},{80,96},{96,112},{112,128},... | collective-permute-start | bytes 73736 | tf_op jit(solution)/shard_map/while/body/eval_jaxpr/ppermute | solution.py:42
  372.5 7.5 %collective-permute-start.2 = (f32[2,4,768]{2,1,0:T(4,128)S(1)}, f32[2,4,768]{2,1,0:T(4,128)S(1)}, u32[]{:S(2)}, u32[]{:S(2)}) collective-permute-start(f32[2,4,768]{2,1,0:T(4,128)S(1)} %maximum_add_fusion.10), channel_id=1, source_target_pairs={{0,16},{16,32},{32,48},{48,64},{64,80},{80,96},{96,112},{112,128},... | collective-permute-start | bytes 73736 | tf_op jit(solution)/shard_map/while/body/eval_jaxpr/ppermute | solution.py:42
  380.9 8.1 %collective-permute-start.3 = (f32[2,4,768]{2,1,0:T(4,128)S(1)}, f32[2,4,768]{2,1,0:T(4,128)S(1)}, u32[]{:S(2)}, u32[]{:S(2)}) collective-permute-start(f32[2,4,768]{2,1,0:T(4,128)S(1)} %maximum_add_fusion.11), channel_id=1, source_target_pairs={{16,0},{32,16},{48,32},{64,48},{80,64},{96,80},{112,96},{128,112},... | collective-permute-start | bytes 73736 | tf_op jit(solution)/shard_map/while/body/eval_jaxpr/ppermute | solution.py:42
  389.1 7.5 %collective-permute-start.3 = (f32[2,4,768]{2,1,0:T(4,128)S(1)}, f32[2,4,768]{2,1,0:T(4,128)S(1)}, u32[]{:S(2)}, u32[]{:S(2)}) collective-permute-start(f32[2,4,768]{2,1,0:T(4,128)S(1)} %maximum_add_fusion.11), channel_id=1, source_target_pairs={{16,0},{32,16},{48,32},{64,48},{80,64},{96,80},{112,96},{128,112},... | collective-permute-start | bytes 73736 | tf_op jit(solution)/shard_map/while/body/eval_jaxpr/ppermute | solution.py:42
  396.7 7.5 %collective-permute-start.3 = (f32[2,4,768]{2,1,0:T(4,128)S(1)}, f32[2,4,768]{2,1,0:T(4,128)S(1)}, u32[]{:S(2)}, u32[]{:S(2)}) collective-permute-start(f32[2,4,768]{2,1,0:T(4,128)S(1)} %maximum_add_fusion.11), channel_id=1, source_target_pairs={{16,0},{32,16},{48,32},{64,48},{80,64},{96,80},{112,96},{128,112},... | collective-permute-start | bytes 73736 | tf_op jit(solution)/shard_map/while/body/eval_jaxpr/ppermute | solution.py:42
  404.4 7.5 %collective-permute-start.3 = (f32[2,4,768]{2,1,0:T(4,128)S(1)}, f32[2,4,768]{2,1,0:T(4,128)S(1)}, u32[]{:S(2)}, u32[]{:S(2)}) collective-permute-start(f32[2,4,768]{2,1,0:T(4,128)S(1)} %maximum_add_fusion.11), channel_id=1, source_target_pairs={{16,0},{32,16},{48,32},{64,48},{80,64},{96,80},{112,96},{128,112},... | collective-permute-start | bytes 73736 | tf_op jit(solution)/shard_map/while/body/eval_jaxpr/ppermute | solution.py:42
  412.0 7.5 %collective-permute-start.3 = (f32[2,4,768]{2,1,0:T(4,128)S(1)}, f32[2,4,768]{2,1,0:T(4,128)S(1)}, u32[]{:S(2)}, u32[]{:S(2)}) collective-permute-start(f32[2,4,768]{2,1,0:T(4,128)S(1)} %maximum_add_fusion.11), channel_id=1, source_target_pairs={{16,0},{32,16},{48,32},{64,48},{80,64},{96,80},{112,96},{128,112},... | collective-permute-start | bytes 73736 | tf_op jit(solution)/shard_map/while/body/eval_jaxpr/ppermute | solution.py:42
  419.6 7.5 %collective-permute-start.3 = (f32[2,4,768]{2,1,0:T(4,128)S(1)}, f32[2,4,768]{2,1,0:T(4,128)S(1)}, u32[]{:S(2)}, u32[]{:S(2)}) collective-permute-start(f32[2,4,768]{2,1,0:T(4,128)S(1)} %maximum_add_fusion.11), channel_id=1, source_target_pairs={{16,0},{32,16},{48,32},{64,48},{80,64},{96,80},{112,96},{128,112},... | collective-permute-start | bytes 73736 | tf_op jit(solution)/shard_map/while/body/eval_jaxpr/ppermute | solution.py:42
  427.3 7.5 %collective-permute-start.3 = (f32[2,4,768]{2,1,0:T(4,128)S(1)}, f32[2,4,768]{2,1,0:T(4,128)S(1)}, u32[]{:S(2)}, u32[]{:S(2)}) collective-permute-start(f32[2,4,768]{2,1,0:T(4,128)S(1)} %maximum_add_fusion.11), channel_id=1, source_target_pairs={{16,0},{32,16},{48,32},{64,48},{80,64},{96,80},{112,96},{128,112},... | collective-permute-start | bytes 73736 | tf_op jit(solution)/shard_map/while/body/eval_jaxpr/ppermute | solution.py:42
  434.9 7.5 %collective-permute-start.3 = (f32[2,4,768]{2,1,0:T(4,128)S(1)}, f32[2,4,768]{2,1,0:T(4,128)S(1)}, u32[]{:S(2)}, u32[]{:S(2)}) collective-permute-start(f32[2,4,768]{2,1,0:T(4,128)S(1)} %maximum_add_fusion.11), channel_id=1, source_target_pairs={{16,0},{32,16},{48,32},{64,48},{80,64},{96,80},{112,96},{128,112},... | collective-permute-start | bytes 73736 | tf_op jit(solution)/shard_map/while/body/eval_jaxpr/ppermute | solution.py:42
  442.6 7.5 %collective-permute-start.3 = (f32[2,4,768]{2,1,0:T(4,128)S(1)}, f32[2,4,768]{2,1,0:T(4,128)S(1)}, u32[]{:S(2)}, u32[]{:S(2)}) collective-permute-start(f32[2,4,768]{2,1,0:T(4,128)S(1)} %maximum_add_fusion.11), channel_id=1, source_target_pairs={{16,0},{32,16},{48,32},{64,48},{80,64},{96,80},{112,96},{128,112},... | collective-permute-start | bytes 73736 | tf_op jit(solution)/shard_map/while/body/eval_jaxpr/ppermute | solution.py:42
  450.2 7.5 %collective-permute-start.3 = (f32[2,4,768]{2,1,0:T(4,128)S(1)}, f32[2,4,768]{2,1,0:T(4,128)S(1)}, u32[]{:S(2)}, u32[]{:S(2)}) collective-permute-start(f32[2,4,768]{2,1,0:T(4,128)S(1)} %maximum_add_fusion.11), channel_id=1, source_target_pairs={{16,0},{32,16},{48,32},{64,48},{80,64},{96,80},{112,96},{128,112},... | collective-permute-start | bytes 73736 | tf_op jit(solution)/shard_map/while/body/eval_jaxpr/ppermute | solution.py:42
  457.8 7.5 %collective-permute-start.3 = (f32[2,4,768]{2,1,0:T(4,128)S(1)}, f32[2,4,768]{2,1,0:T(4,128)S(1)}, u32[]{:S(2)}, u32[]{:S(2)}) collective-permute-start(f32[2,4,768]{2,1,0:T(4,128)S(1)} %maximum_add_fusion.11), channel_id=1, source_target_pairs={{16,0},{32,16},{48,32},{64,48},{80,64},{96,80},{112,96},{128,112},... | collective-permute-start | bytes 73736 | tf_op jit(solution)/shard_map/while/body/eval_jaxpr/ppermute | solution.py:42
  465.5 7.5 %collective-permute-start.3 = (f32[2,4,768]{2,1,0:T(4,128)S(1)}, f32[2,4,768]{2,1,0:T(4,128)S(1)}, u32[]{:S(2)}, u32[]{:S(2)}) collective-permute-start(f32[2,4,768]{2,1,0:T(4,128)S(1)} %maximum_add_fusion.11), channel_id=1, source_target_pairs={{16,0},{32,16},{48,32},{64,48},{80,64},{96,80},{112,96},{128,112},... | collective-permute-start | bytes 73736 | tf_op jit(solution)/shard_map/while/body/eval_jaxpr/ppermute | solution.py:42
  473.1 7.5 %collective-permute-start.3 = (f32[2,4,768]{2,1,0:T(4,128)S(1)}, f32[2,4,768]{2,1,0:T(4,128)S(1)}, u32[]{:S(2)}, u32[]{:S(2)}) collective-permute-start(f32[2,4,768]{2,1,0:T(4,128)S(1)} %maximum_add_fusion.11), channel_id=1, source_target_pairs={{16,0},{32,16},{48,32},{64,48},{80,64},{96,80},{112,96},{128,112},... | collective-permute-start | bytes 73736 | tf_op jit(solution)/shard_map/while/body/eval_jaxpr/ppermute | solution.py:42
  480.7 7.5 %collective-permute-start.3 = (f32[2,4,768]{2,1,0:T(4,128)S(1)}, f32[2,4,768]{2,1,0:T(4,128)S(1)}, u32[]{:S(2)}, u32[]{:S(2)}) collective-permute-start(f32[2,4,768]{2,1,0:T(4,128)S(1)} %maximum_add_fusion.11), channel_id=1, source_target_pairs={{16,0},{32,16},{48,32},{64,48},{80,64},{96,80},{112,96},{128,112},... | collective-permute-start | bytes 73736 | tf_op jit(solution)/shard_map/while/body/eval_jaxpr/ppermute | solution.py:42
  488.4 7.5 %collective-permute-start.3 = (f32[2,4,768]{2,1,0:T(4,128)S(1)}, f32[2,4,768]{2,1,0:T(4,128)S(1)}, u32[]{:S(2)}, u32[]{:S(2)}) collective-permute-start(f32[2,4,768]{2,1,0:T(4,128)S(1)} %maximum_add_fusion.11), channel_id=1, source_target_pairs={{16,0},{32,16},{48,32},{64,48},{80,64},{96,80},{112,96},{128,112},... | collective-permute-start | bytes 73736 | tf_op jit(solution)/shard_map/while/body/eval_jaxpr/ppermute | solution.py:42
  (58 other events, 431.1 us)
where the time goes:
time: 507 us; the launch traced here: 503 us
  starting transfers between devices  281 us (55%)
  waiting for transfers between devices  196 us (39%)
  matrix products  9.93 us (2%)
  local copies, waits for them, and re-layouts  7.83 us (2%)
  other arithmetic  6.05 us (1%)
    ppermute x60, starting transfers between devices, passed_along(): lax.ppermute(value, axis, [(source, source + steps) for source in range(l...  269 us
    ppermute x60, waiting for transfers between devices, passed_along(): lax.ppermute(value, axis, [(source, source + steps) for source in range(l...  186 us
  transfers between devices with their start and end apart: 64, of which 62 were waited for; matrix products, arithmetic and copies ran while one was open for 0% of the time, Pallas kernels for 0%

commit v1 on v0

v1 whole, which is shorter than its diff:
```python
import functools
import math

import jax
import jax.numpy as jnp
import numpy as np
from jax import lax
from jax.experimental import pallas as pl
from jax.experimental.pallas import tpu as pltpu
from jax.sharding import PartitionSpec as P

SCALES = (128, 256)
DER_FIRST = (1.0 / 280, -4.0 / 105, 1.0 / 5, -4.0 / 5, 0.0, 4.0 / 5, -1.0 / 5, 4.0 / 105, -1.0 / 280)
DER_SECOND = (-1.0 / 560, 8.0 / 315, -1.0 / 5, 8.0 / 5, -205.0 / 72, 8.0 / 5, -1.0 / 5, 8.0 / 315, -1.0 / 560)
DER_NONE = (0.0, 0.0, 0.0, 0.0, 1.0, 0.0, 0.0, 0.0, 0.0)
DERS = (DER_NONE, DER_FIRST, DER_SECOND)
DERICHE_POLES = ((1.68, 3.735, 1.783, 0.6318), (-0.6803, -0.2598, 1.723, 1.997))
FEATURES = ((0, 0), (0, 1), (1, 0), (0, 2), (1, 1), (2, 0))
N = 128
EXT = 64
MESH = pl.DeviceIdType.MESH


def poles(deviation):
    total = 0.0
    for cw, sw, decay, freq in DERICHE_POLES:
        z = np.exp(complex(-decay, freq) / deviation)
        q = z / (1.0 - z)
        total += cw + 2.0 * (cw * q.real + sw * q.imag)
    return [
        (complex(cw, -sw) / total, np.exp(complex(-decay, freq) / deviation))
        for cw, sw, decay, freq in DERICHE_POLES
    ]


def kernel_values(deviation, offsets):
    offsets = np.abs(np.asarray(offsets, dtype=np.float64))
    return sum((a * z**offsets).real for a, z in poles(deviation))


def summary_table():
    table = np.zeros((24, N))
    n = np.arange(N)
    row = 0
    for s in SCALES:
        for _, z in poles(s):
            causal, anti = z ** (N - 1 - n), z**n
            table[row], table[row + 1] = causal.real, causal.imag
            table[16 + row], table[17 + row] = anti.real, anti.imag
            row += 2
    for k in range(4):
        table[8 + k, k] = 1.0
        table[12 + k, N - 4 + k] = 1.0
    return table


def combine_table(count):
    table = np.zeros((count, EXT, count * 16))
    for pos in range(count):
        w = table[pos]
        for k in range(4):
            if pos > 0:
                w[k, (pos - 1) * 16 + 8 + 4 + k] = 1.0
            if pos < count - 1:
                w[4 + k, (pos + 1) * 16 + k] = 1.0
        for si, s in enumerate(SCALES):
            for ai, der in enumerate(DERS):
                for pi, (_, z) in enumerate(poles(s)):
                    up = 8 + (si * 3 + ai) * 8 + pi * 2
                    down = up + 4
                    col = si * 4 + pi * 2
                    dz = sum(der[t + 4] * z**t for t in range(-4, 5))
                    dinv = sum(der[t + 4] * z ** (-t) for t in range(-4, 5))
                    for src in range(count):
                        if src < pos:
                            g = dz * z ** (N * (pos - 1 - src))
                            at = src * 16 + col
                            w[up, at], w[up, at + 1] = g.real, -g.imag
                            w[up + 1, at], w[up + 1, at + 1] = g.imag, g.real
                        if src > pos:
                            g = dinv * z ** (N * (src - pos - 1))
                            at = src * 16 + 8 + col
                            w[down, at], w[down, at + 1] = g.real, -g.imag
                            w[down + 1, at], w[down + 1, at + 1] = g.imag, g.real
                    first = 8
                    last = (count - 1) * 16 + (8 + 4 if pos == count - 1 else 4)
                    for n in range(4):
                        g = -sum(
                            der[n - m + 4] * z ** (N * pos - 1 - m)
                            for m in range(-4, 0)
                            if -4 <= n - m <= 4
                        )
                        w[up, first + n] += g.real
                        w[up + 1, first + n] += g.imag
                        g = -sum(
                            der[n - 4 - m + 4] * z ** (N * (count - 1 - pos) + m)
                            for m in range(0, 4)
                            if -4 <= n - 4 - m <= 4
                        )
                        w[down, last + n] += g.real
                        w[down + 1, last + n] += g.imag
    return table


def filter_tables():
    local = np.zeros((6, N, N))
    ext = np.zeros((6, N, EXT))
    c = np.arange(N)
    for si, s in enumerate(SCALES):
        base = 2.0 * math.sqrt(math.pi) * s
        for ai, der in enumerate(DERS):
            k = si * 3 + ai
            factor = math.sqrt(base) * float(s) ** ai

            def kappa(d):
                return sum(der[t + 4] * kernel_values(s, d + t) for t in range(-4, 5))

            local[k] = kappa(c[:, None] - c[None, :])
            for n in range(4):
                up, down = n - 4, N + n
                ext[k, :, n] = kappa(c - up)
                ext[k, :, 4 + n] = kappa(c - down)
                for a, z in poles(s):
                    dz = sum(der[t + 4] * z**t for t in range(-4, 5))
                    dinv = sum(der[t + 4] * z ** (-t) for t in range(-4, 5))
                    ext[k, :, n] -= (a * dz * z ** (c - up + 0.0)).real
                    ext[k, :, 4 + n] -= (a * dinv * z ** (down - c + 0.0)).real
                ext[k, 4:, n] = 0.0
                ext[k, : N - 4, 4 + n] = 0.0
            for pi, (a, z) in enumerate(poles(s)):
                up = 8 + k * 8 + pi * 2
                g = a * z ** (c + 1.0)
                ext[k, :, up], ext[k, :, up + 1] = g.real, -g.imag
                g = a * z ** (N - c + 0.0)
                ext[k, :, up + 4], ext[k, :, up + 5] = g.real, -g.imag
            local[k] *= factor
            ext[k] *= factor
    return local.reshape(6 * N, N), ext.reshape(6 * N, EXT)


def halves(table):
    table = np.asarray(table, dtype=np.float32)
    high = table.astype(jnp.bfloat16)
    low = (table - high.astype(np.float32)).astype(jnp.bfloat16)
    return np.stack([high, low])


def split(x):
    high = x.astype(jnp.bfloat16)
    return high, (x - high.astype(jnp.float32)).astype(jnp.bfloat16)


def mm(a, b, rhs_lanes=False):
    dims = (((1,), (1 if rhs_lanes else 0,)), ((), ()))

    def one(x, y):
        return lax.dot_general(x, y, dims, preferred_element_type=jnp.float32)

    return one(a[0], b[0]) + (one(a[0], b[1]) + one(a[1], b[0]))


def kernel(
    count,
    x_hbm,
    m_hbm,
    loc_hbm,
    ext_hbm,
    comb_hbm,
    o_hbm,
    x_ref,
    m_ref,
    loc_ref,
    ext_ref,
    cv_ref,
    ch_ref,
    fold_ref,
    pv_ref,
    ph_ref,
    pb_ref,
    gv_ref,
    gh_ref,
    gb_ref,
    tloc_ref,
    acc_ref,
    o_ref,
    in_sems,
    out_sems,
    send_sems,
    recv_sems,
):
    me_r, me_c = lax.axis_index("row"), lax.axis_index("col")
    span = count * 16

    barrier = pltpu.get_barrier_semaphore()
    for d in range(1, count):
        pl.semaphore_signal(barrier, inc=1, device_id=(lax.rem(me_r + d, count), me_c), device_id_type=MESH)
        pl.semaphore_signal(barrier, inc=1, device_id=(me_r, lax.rem(me_c + d, count)), device_id_type=MESH)

    loads = [
        pltpu.make_async_copy(src, dst, in_sems.at[k])
        for k, (src, dst) in enumerate(
            (
                (x_hbm, x_ref),
                (m_hbm, m_ref),
                (comb_hbm.at[me_c], ch_ref),
                (ext_hbm, ext_ref),
                (comb_hbm.at[me_r], cv_ref),
                (loc_hbm, loc_ref),
            )
        )
    ]
    for load in loads:
        load.start()

    loads[0].wait()
    loads[1].wait()
    x = split(x_ref[...])
    m = (m_ref[0], m_ref[1])
    pv = mm(m, x)
    ph = mm(m, x, True)
    pv_ref[...] = pv
    ph_ref[...] = ph
    gv_ref[pl.ds(pl.multiple_of(me_r * 16, 16), 16), :] = pv[:16]
    gh_ref[pl.ds(pl.multiple_of(me_c * 16, 16), 16), :] = ph[:16]

    def message(kind, d, src, dst):
        me = me_r if kind == 0 else me_c
        to = lax.rem(me + d, count)
        off = pl.multiple_of(((me + d) // count) * 8, 8)
        return pltpu.make_async_remote_copy(
            src_ref=src.at[pl.ds(off, 16)],
            dst_ref=dst.at[pl.ds(pl.multiple_of(me * 16, 16), 16)],
            send_sem=send_sems.at[kind, d],
            recv_sem=recv_sems.at[kind, d],
            device_id=(to, me_c) if kind == 0 else (me_r, to),
            device_id_type=MESH,
        )

    order = sorted(range(1, count), key=lambda d: -min(d, count - d))
    down = [message(0, d, pv_ref, gv_ref) for d in order]
    across = [message(1, d, ph_ref, gh_ref) for d in order]

    pl.semaphore_wait(barrier, 2 * (count - 1))
    for copy in down:
        copy.start()
    for copy in across:
        copy.start()

    for k in (2, 3):
        loads[k].wait()
    ext_t = (ext_ref[0], ext_ref[1])
    fold = split(mm(ext_t, (ch_ref[0], ch_ref[1])))
    fold_ref[0], fold_ref[1] = fold
    loads[4].wait()
    loads[5].wait()
    loc_t = (loc_ref[0], loc_ref[1])
    tloc_ref[...] = mm(loc_t, x, True)

    for copy in down:
        copy.wait_recv()
    lines = split(mm((cv_ref[0], cv_ref[1]), split(gv_ref[...])))
    pb = mm(m, lines, True)
    pb = jnp.concatenate([pb, jnp.zeros((24, 128 - EXT), jnp.float32)], axis=1)
    pb_ref[...] = pb
    gb_ref[pl.ds(pl.multiple_of(me_c * 16, 16), 16), :] = pb[:16]
    corner = [message(2, d, pb_ref, gb_ref) for d in order]
    for copy in corner:
        copy.start()

    text = mm(loc_t, lines, True)
    for copy in across:
        copy.wait_recv()
    fold_t = (fold_ref[0], fold_ref[1])
    tloc = tloc_ref[...] + mm(fold_t, split(gh_ref[...]))
    for level in range(2):
        for f, (a, b) in enumerate(FEATURES):
            rows = slice((level * 3 + a) * N, (level * 3 + a + 1) * N)
            cols = slice((level * 3 + b) * N, (level * 3 + b + 1) * N)
            acc_ref[level * 6 + f] = mm((loc_ref[0, rows], loc_ref[1, rows]), split(tloc[cols]), True)

    for copy in corner:
        copy.wait_recv()
    text = text + mm(fold_t, split(gb_ref[...][:, :EXT]))
    outs = []
    for level in range(2):
        for f, (a, b) in enumerate(FEATURES):
            rows = slice((level * 3 + a) * N, (level * 3 + a + 1) * N)
            cols = slice((level * 3 + b) * N, (level * 3 + b + 1) * N)
            k = level * 6 + f
            full = acc_ref[k] + mm((ext_ref[0, rows], ext_ref[1, rows]), split(text[cols]), True)
            o_ref[k] = full.astype(jnp.bfloat16)
            copy = pltpu.make_async_copy(o_ref.at[k], o_hbm.at[k], out_sems.at[k])
            copy.start()
            outs.append(copy)
    for copy in outs:
        copy.wait()
    for copy in down + across + corner:
        copy.wait_send()


def on_device(count, tables, image):
    local, ext, summary, comb = tables
    f32, bf16 = jnp.float32, jnp.bfloat16
    span = count * 16
    return pl.pallas_call(
        functools.partial(kernel, count),
        out_shape=jax.ShapeDtypeStruct((12, N, N), bf16),
        in_specs=[pl.BlockSpec(memory_space=pl.ANY)] * 5,
        out_specs=pl.BlockSpec(memory_space=pl.ANY),
        scratch_shapes=[
            pltpu.VMEM((N, N), f32),
            pltpu.VMEM((2, 24, N), bf16),
            pltpu.VMEM((2, 6 * N, N), bf16),
            pltpu.VMEM((2, 6 * N, EXT), bf16),
            pltpu.VMEM((2, EXT, span), bf16),
            pltpu.VMEM((2, EXT, span), bf16),
            pltpu.VMEM((2, 6 * N, span), bf16),
            pltpu.VMEM((24, N), f32),
            pltpu.VMEM((24, N), f32),
            pltpu.VMEM((24, N), f32),
            pltpu.VMEM((span, N), f32),
            pltpu.VMEM((span, N), f32),
            pltpu.VMEM((span, N), f32),
            pltpu.VMEM((6 * N, N), f32),
            pltpu.VMEM((12, N, N), f32),
            pltpu.VMEM((12, N, N), bf16),
            pltpu.SemaphoreType.DMA((6,)),
            pltpu.SemaphoreType.DMA((12,)),
            pltpu.SemaphoreType.DMA((3, count)),
            pltpu.SemaphoreType.DMA((3, count)),
        ],
        compiler_params=pltpu.CompilerParams(collective_id=0, has_side_effects=True),
    )(image, jnp.asarray(summary), jnp.asarray(local), jnp.asarray(ext), jnp.asarray(comb))


def solution(mesh):
    count = mesh.shape["row"]
    local, ext = filter_tables()
    tables = (
        halves(local),
        halves(ext),
        halves(summary_table()),
        halves(combine_table(count)).swapaxes(0, 1),
    )
    return jax.shard_map(
        functools.partial(on_device, count, tables),
        mesh=mesh,
        in_specs=(P("row", "col"),),
        out_specs=P(None, "row", "col"),
        check_vma=False,
    )
```

time: 507 us -> 26 us (0.05)
  the two profiles are of different devices: /device:TPU:121 before, /device:TPU:8 now
where the time goes in v1:
time: 26 us; the launch traced here: 25.8 us
  Pallas kernels  24.1 us (93%)
  local copies, waits for them, and re-layouts  1.77 us (7%)
    pallas_call x1, Pallas kernels, on_device(): pl.pallas_call(functools.partial(kernel, count), out_shape=jax.ShapeDtype...  24.1 us
    unnamed x1, local copies, waits for them, and re-layouts  1.77 us

profile of v1, /device:TPU:8, one launch (start us, length us, event | category | flops | bytes accessed | tf_op | source)
XLA Modules:
  0.0 25.8 jit_solution(4487769550289927168)
XLA Ops:
  0.0 24.1 %shard_map.55 = bf16[12,128,128]{2,1,0:T(8,128)(2,1)} custom-call(f32[128,128]{1,0:T(8,128)} %x_hbm.1, bf16[2,24,128]{2,1,0:T(8,128)(2,1)} %constant.8.clone.m_hbm, bf16[2,768,128]{2,1,0:T(8,128)(2,1)} %constant.9.clone.loc_hbm, bf16[2,768,64]{2,1,0:T(8,128)(2,1)} %constant.10.clone.ext_hbm, bf16[16,2,64,256]{3,2,1,0:T(8,128)(2,1)} %constant.11.clone.comb_hbm), custom_call_target="tpu_custom_call" | custom-call | tf_op jit(solution)/shard_map/pallas_call | solution.py:305
  24.1 1.8 %copy.7 = bf16[12,128,128]{2,1,0:T(8,128)(2,1)} copy(bf16[12,128,128]{2,1,0:T(8,128)(2,1)} %shard_map.55) | data formatting | bytes 786432

commit v2 on v1

--- a/solution.py
+++ b/solution.py
@@ -142,7 +142,24 @@
     table = np.asarray(table, dtype=np.float32)
     high = table.astype(jnp.bfloat16)
     low = (table - high.astype(np.float32)).astype(jnp.bfloat16)
-    return np.stack([high, low])
+    return high, low
+
+
+def packed_table(count):
+    local, ext = (halves(t) for t in filter_tables())
+    summary = halves(np.pad(summary_table(), ((0, 8), (0, 0))))
+    comb = halves(combine_table(count))
+    return np.concatenate(
+        [
+            np.concatenate(summary, axis=1),
+            np.concatenate(local, axis=1),
+            np.concatenate([ext[0], ext[0], ext[1], ext[1]], axis=1),
+            np.concatenate(comb, axis=1).reshape(count * 2 * EXT, count * 16),
+        ]
+    )
+
+
+LOC_AT, EXT_AT, COMB_AT = 32, 32 + 6 * N, 32 + 12 * N
 
 
 def split(x):
@@ -150,200 +167,240 @@
     return high, (x - high.astype(jnp.float32)).astype(jnp.bfloat16)
 
 
+def dot(a, b, rhs_lanes=False):
+    dims = (((1,), (1 if rhs_lanes else 0,)), ((), ()))
+    return lax.dot_general(a, b, dims, preferred_element_type=jnp.float32)
+
+
 def mm(a, b, rhs_lanes=False):
-    dims = (((1,), (1 if rhs_lanes else 0,)), ((), ()))
-
-    def one(x, y):
-        return lax.dot_general(x, y, dims, preferred_element_type=jnp.float32)
-
-    return one(a[0], b[0]) + (one(a[0], b[1]) + one(a[1], b[0]))
+    return dot(a[0], b[0], rhs_lanes) + (dot(a[0], b[1], rhs_lanes) + dot(a[1], b[0], rhs_lanes))
 
 
 def kernel(
     count,
     x_hbm,
-    m_hbm,
-    loc_hbm,
-    ext_hbm,
-    comb_hbm,
-    o_hbm,
+    tab_hbm,
+    o_ref,
     x_ref,
     m_ref,
     loc_ref,
     ext_ref,
     cv_ref,
     ch_ref,
-    fold_ref,
     pv_ref,
     ph_ref,
     pb_ref,
     gv_ref,
     gh_ref,
     gb_ref,
-    tloc_ref,
     acc_ref,
-    o_ref,
     in_sems,
-    out_sems,
     send_sems,
     recv_sems,
+    late_sem,
+    row_sem,
+    ok_sems,
 ):
     me_r, me_c = lax.axis_index("row"), lax.axis_index("col")
+    part = count // 2
+    half, spot = me_c // part, lax.rem(me_c, part)
     span = count * 16
 
+    def load(k, src, dst):
+        return pltpu.make_async_copy(src, dst, in_sems.at[k])
+
+    def comb_at(pos):
+        return tab_hbm.at[pl.ds(pl.multiple_of(COMB_AT + pos * 2 * EXT, 16), 2 * EXT)]
+
+    loads = [
+        load(0, x_hbm, x_ref),
+        load(1, tab_hbm.at[pl.ds(0, 32)], m_ref),
+        load(2, comb_at(me_r), cv_ref),
+        load(3, tab_hbm.at[pl.ds(LOC_AT, 6 * N)], loc_ref),
+        load(4, tab_hbm.at[pl.ds(EXT_AT, 6 * N)], ext_ref),
+        load(5, comb_at(me_c), ch_ref),
+    ]
+    for copy in loads:
+        copy.start()
+
+    def near(d):
+        return half * part + lax.rem(spot + d, part)
+
+    def far(d):
+        return (1 - half) * part + lax.rem(spot + d, part)
+
     barrier = pltpu.get_barrier_semaphore()
-    for d in range(1, count):
-        pl.semaphore_signal(barrier, inc=1, device_id=(lax.rem(me_r + d, count), me_c), device_id_type=MESH)
-        pl.semaphore_signal(barrier, inc=1, device_id=(me_r, lax.rem(me_c + d, count)), device_id_type=MESH)
-
-    loads = [
-        pltpu.make_async_copy(src, dst, in_sems.at[k])
-        for k, (src, dst) in enumerate(
-            (
-                (x_hbm, x_ref),
-                (m_hbm, m_ref),
-                (comb_hbm.at[me_c], ch_ref),
-                (ext_hbm, ext_ref),
-                (comb_hbm.at[me_r], cv_ref),
-                (loc_hbm, loc_ref),
-            )
+
+    def greet(sem, row, col):
+        pl.semaphore_signal(sem, inc=1, device_id=(row, col), device_id_type=MESH)
+
+    @pl.when(half == 0)
+    def _():
+        for d in range(part):
+            greet(barrier, me_r, far(d))
+        for d in range(1, part):
+            greet(barrier, me_r, near(d))
+        for d in range(1, count):
+            greet(barrier, lax.rem(me_r + d, count), me_c)
+
+    @pl.when(half == 1)
+    def _():
+        pl.semaphore_wait(barrier, part)
+        for d in range(part):
+            greet(late_sem, me_r, far(d))
+
+    def message(kind, k, to, src, dst):
+        me = me_c if kind == 0 else me_r
+        off = pl.multiple_of(((me - to + count - 1) // count) * 8, 8)
+        return pltpu.make_async_remote_copy(
+            src_ref=src.at[pl.ds(off, 16)],
+            dst_ref=dst.at[pl.ds(pl.multiple_of(me * 16, 16), 16)],
+            send_sem=send_sems.at[kind, k],
+            recv_sem=recv_sems.at[kind, k],
+            device_id=(me_r, to) if kind == 0 else (to, me_c),
+            device_id_type=MESH,
         )
-    ]
-    for load in loads:
-        load.start()
+
+    across_near = [message(0, d, near(d), ph_ref, gh_ref) for d in range(1, part)]
+    across_far = [message(0, part + d, far(d), ph_ref, gh_ref) for d in range(part)]
+    order = sorted(range(1, count), key=lambda d: -min(d, count - d))
+    down = [message(1, d, lax.rem(me_r + d, count), pv_ref, gv_ref) for d in order]
+    corner = [message(2, d, lax.rem(me_r + d, count), pb_ref, gb_ref) for d in order]
 
     loads[0].wait()
     loads[1].wait()
     x = split(x_ref[...])
-    m = (m_ref[0], m_ref[1])
+    m = (m_ref[:24, :N], m_ref[:24, N:])
+    ph = mm(m, x, True)
+    ph_ref[...] = ph
+    gh_ref[pl.ds(pl.multiple_of(me_c * 16, 16), 16), :] = ph[:16]
     pv = mm(m, x)
-    ph = mm(m, x, True)
     pv_ref[...] = pv
-    ph_ref[...] = ph
     gv_ref[pl.ds(pl.multiple_of(me_r * 16, 16), 16), :] = pv[:16]
-    gh_ref[pl.ds(pl.multiple_of(me_c * 16, 16), 16), :] = ph[:16]
-
-    def message(kind, d, src, dst):
-        me = me_r if kind == 0 else me_c
-        to = lax.rem(me + d, count)
-        off = pl.multiple_of(((me + d) // count) * 8, 8)
-        return pltpu.make_async_remote_copy(
-            src_ref=src.at[pl.ds(off, 16)],
-            dst_ref=dst.at[pl.ds(pl.multiple_of(me * 16, 16), 16)],
-            send_sem=send_sems.at[kind, d],
-            recv_sem=recv_sems.at[kind, d],
-            device_id=(to, me_c) if kind == 0 else (me_r, to),
-            device_id_type=MESH,
-        )
-
-    order = sorted(range(1, count), key=lambda d: -min(d, count - d))
-    down = [message(0, d, pv_ref, gv_ref) for d in order]
-    across = [message(1, d, ph_ref, gh_ref) for d in order]
-
-    pl.semaphore_wait(barrier, 2 * (count - 1))
-    for copy in down:
+
+    mirror = count - 2 - me_c // 2 * 2 + lax.rem(me_c, 2)
+
+    @pl.when(half == 0)
+    def _():
+        pl.semaphore_wait(barrier, count - 1 + part - 1)
+        for copy in across_near:
+            copy.start()
+        for copy in down:
+            copy.start()
+        pl.semaphore_wait(late_sem, part)
+        greet(ok_sems.at[0], me_r, mirror)
+        for d in range(1, count):
+            greet(row_sem, lax.rem(me_r + d, count), me_c)
+        for copy in across_far:
+            copy.start()
+        pl.semaphore_wait(row_sem, count - 1)
+        greet(ok_sems.at[1], me_r, mirror)
+
+    @pl.when(half == 1)
+    def _():
+        for copy in across_far:
+            copy.start()
+        pl.semaphore_wait(ok_sems.at[0], 1)
+        for copy in across_near:
+            copy.start()
+        pl.semaphore_wait(ok_sems.at[1], 1)
+        for copy in down:
+            copy.start()
+
+    def stacked(v):
+        return jnp.concatenate([v[0], v[1], v[0], v[1]], axis=0)
+
+    def combine(c_ref, g_ref):
+        return mm((c_ref[:EXT], c_ref[EXT:]), split(g_ref[...]))
+
+    loads[5].wait()
+    for copy in across_near + across_far:
+        copy.wait_recv()
+    lines = combine(ch_ref, gh_ref)
+    lines = split(jnp.concatenate([lines, lines], axis=0))
+    pb = mm(m, lines, True)
+    pb_ref[...] = pb
+    gb_ref[pl.ds(pl.multiple_of(me_r * 16, 16), 16), :] = pb[:16]
+    for copy in corner:
         copy.start()
-    for copy in across:
-        copy.start()
-
-    for k in (2, 3):
+    for k in (2, 3, 4):
         loads[k].wait()
-    ext_t = (ext_ref[0], ext_ref[1])
-    fold = split(mm(ext_t, (ch_ref[0], ch_ref[1])))
-    fold_ref[0], fold_ref[1] = fold
-    loads[4].wait()
-    loads[5].wait()
-    loc_t = (loc_ref[0], loc_ref[1])
-    tloc_ref[...] = mm(loc_t, x, True)
-
+    filtered = dot(loc_ref[...], jnp.concatenate([x[0], x[0]], axis=0)) + dot(loc_ref[:, :N], x[1])
     for copy in down:
         copy.wait_recv()
-    lines = split(mm((cv_ref[0], cv_ref[1]), split(gv_ref[...])))
-    pb = mm(m, lines, True)
-    pb = jnp.concatenate([pb, jnp.zeros((24, 128 - EXT), jnp.float32)], axis=1)
-    pb_ref[...] = pb
-    gb_ref[pl.ds(pl.multiple_of(me_c * 16, 16), 16), :] = pb[:16]
-    corner = [message(2, d, pb_ref, gb_ref) for d in order]
-    for copy in corner:
-        copy.start()
-
-    text = mm(loc_t, lines, True)
-    for copy in across:
-        copy.wait_recv()
-    fold_t = (fold_ref[0], fold_ref[1])
-    tloc = tloc_ref[...] + mm(fold_t, split(gh_ref[...]))
+    filtered = filtered + dot(ext_ref[...], stacked(split(combine(cv_ref, gv_ref))))
     for level in range(2):
-        for f, (a, b) in enumerate(FEATURES):
-            rows = slice((level * 3 + a) * N, (level * 3 + a + 1) * N)
-            cols = slice((level * 3 + b) * N, (level * 3 + b + 1) * N)
-            acc_ref[level * 6 + f] = mm((loc_ref[0, rows], loc_ref[1, rows]), split(tloc[cols]), True)
-
+        for a in range(3):
+            k = level * 3 + a
+            wide = slice(level * 3 * N, (level * 3 + 3 - a) * N)
+            t = split(filtered[k * N : (k + 1) * N])
+            acc_ref[k, :, : (3 - a) * N] = dot(
+                jnp.concatenate([t[0], t[0]], axis=1), loc_ref[wide], True
+            ) + dot(t[1], loc_ref[wide, :N], True)
+
+    carried = mm((loc_ref[:, :N], loc_ref[:, N:]), lines, True)
     for copy in corner:
         copy.wait_recv()
-    text = text + mm(fold_t, split(gb_ref[...][:, :EXT]))
-    outs = []
+    carried = carried + dot(ext_ref[...], stacked(split(combine(cv_ref, gb_ref))))
+
+    high = carried.astype(jnp.bfloat16).astype(jnp.float32)
+    lane = lax.broadcasted_iota(jnp.int32, carried.shape, 1)
+    pair = jnp.where(lane < EXT, high, carried - high).astype(jnp.bfloat16)
+    pair = jnp.concatenate([pair, pair], axis=1)
     for level in range(2):
-        for f, (a, b) in enumerate(FEATURES):
-            rows = slice((level * 3 + a) * N, (level * 3 + a + 1) * N)
-            cols = slice((level * 3 + b) * N, (level * 3 + b + 1) * N)
-            k = level * 6 + f
-            full = acc_ref[k] + mm((ext_ref[0, rows], ext_ref[1, rows]), split(text[cols]), True)
-            o_ref[k] = full.astype(jnp.bfloat16)
-            copy = pltpu.make_async_copy(o_ref.at[k], o_hbm.at[k], out_sems.at[k])
-            copy.start()
-            outs.append(copy)
-    for copy in outs:
-        copy.wait()
-    for copy in down + across + corner:
+        for a in range(3):
+            k = level * 3 + a
+            wide = slice(level * 3 * N, (level * 3 + 3 - a) * N)
+            full = acc_ref[k, :, : (3 - a) * N] + dot(pair[k * N : (k + 1) * N], ext_ref[wide], True)
+            for b in range(3 - a):
+                f = FEATURES.index((a, b))
+                o_ref[level * 6 + f] = full[:, b * N : (b + 1) * N].astype(jnp.bfloat16)
+    for copy in across_near + across_far + down + corner:
         copy.wait_send()
 
 
-def on_device(count, tables, image):
-    local, ext, summary, comb = tables
+def on_device(count, table, image):
     f32, bf16 = jnp.float32, jnp.bfloat16
     span = count * 16
     return pl.pallas_call(
         functools.partial(kernel, count),
         out_shape=jax.ShapeDtypeStruct((12, N, N), bf16),
-        in_specs=[pl.BlockSpec(memory_space=pl.ANY)] * 5,
-        out_specs=pl.BlockSpec(memory_space=pl.ANY),
+        in_specs=[pl.BlockSpec(memory_space=pl.ANY)] * 2,
+        out_specs=pl.BlockSpec(memory_space=pltpu.VMEM),
         scratch_shapes=[
             pltpu.VMEM((N, N), f32),
-            pltpu.VMEM((2, 24, N), bf16),
-            pltpu.VMEM((2, 6 * N, N), bf16),
-            pltpu.VMEM((2, 6 * N, EXT), bf16),
-            pltpu.VMEM((2, EXT, span), bf16),
-            pltpu.VMEM((2, EXT, span), bf16),
-            pltpu.VMEM((2, 6 * N, span), bf16),
+            pltpu.VMEM((32, 256), bf16),
+            pltpu.VMEM((6 * N, 256), bf16),
+            pltpu.VMEM((6 * N, 256), bf16),
+            pltpu.VMEM((2 * EXT, span), bf16),
+            pltpu.VMEM((2 * EXT, span), bf16),
             pltpu.VMEM((24, N), f32),
             pltpu.VMEM((24, N), f32),
             pltpu.VMEM((24, N), f32),
             pltpu.VMEM((span, N), f32),
             pltpu.VMEM((span, N), f32),
             pltpu.VMEM((span, N), f32),
-            pltpu.VMEM((6 * N, N), f32),
-            pltpu.VMEM((12, N, N), f32),
-            pltpu.VMEM((12, N, N), bf16),
+            pltpu.VMEM((6, N, 3 * N), f32),
             pltpu.SemaphoreType.DMA((6,)),
-            pltpu.SemaphoreType.DMA((12,)),
             pltpu.SemaphoreType.DMA((3, count)),
             pltpu.SemaphoreType.DMA((3, count)),
+            pltpu.SemaphoreType.REGULAR,
+            pltpu.SemaphoreType.REGULAR,
+            pltpu.SemaphoreType.REGULAR((2,)),
         ],
-        compiler_params=pltpu.CompilerParams(collective_id=0, has_side_effects=True),
-    )(image, jnp.asarray(summary), jnp.asarray(local), jnp.asarray(ext), jnp.asarray(comb))
+        compiler_params=pltpu.CompilerParams(
+            collective_id=0, has_side_effects=True, vmem_limit_bytes=VMEM_LIMIT
+        ),
+    )(image, jnp.asarray(table))
+
+
+VMEM_LIMIT = 54000 << 10
 
 
 def solution(mesh):
     count = mesh.shape["row"]
-    local, ext = filter_tables()
-    tables = (
-        halves(local),
-        halves(ext),
-        halves(summary_table()),
-        halves(combine_table(count)).swapaxes(0, 1),
-    )
     return jax.shard_map(
-        functools.partial(on_device, count, tables),
+        functools.partial(on_device, count, packed_table(count)),
         mesh=mesh,
         in_specs=(P("row", "col"),),
         out_specs=P(None, "row", "col"),

time: 26 us -> 23.8 us (0.915)
  the two profiles are of different devices: /device:TPU:8 before, /device:TPU:224 now
where the time goes in v2:
time: 23.8 us; the launch traced here: 23.7 us
  Pallas kernels  22.1 us (93%)
  local copies, waits for them, and re-layouts  1.59 us (7%)
    pallas_call x1, Pallas kernels, on_device(): pl.pallas_call(functools.partial(kernel, count), out_shape=jax.ShapeDtype...  22.1 us
    unnamed x3, local copies, waits for them, and re-layouts  1.59 us

profile of v2, /device:TPU:224, one launch (start us, length us, event | category | flops | bytes accessed | tf_op | source)
XLA Modules:
  0.0 23.7 jit_solution(11060218356545019601)
XLA Ops:
  0.0 0.0 copy-start
  0.0 0.8 %copy-done = f32[128,128]{1,0:T(8,128)S(1)} copy-done((f32[128,128]{1,0:T(8,128)S(1)}, f32[128,128]{1,0:T(8,128)}, u32[]{:S(2)}) %copy-start) | copy-done | bytes 65560
  0.8 22.1 %shard_map.28 = bf16[12,128,128]{2,1,0:T(8,128)(2,1)S(1)} custom-call(f32[128,128]{1,0:T(8,128)S(1)} %copy-done, bf16[3616,256]{1,0:T(8,128)(2,1)} %constant.2.clone.tab_hbm), custom_call_target="tpu_custom_call" | custom-call | tf_op jit(solution)/shard_map/pallas_call | solution.py:365
  22.9 0.7 %copy.4 = bf16[12,128,128]{2,1,0:T(8,128)(2,1)} copy(bf16[12,128,128]{2,1,0:T(8,128)(2,1)S(1)} %shard_map.28) | data formatting | bytes 786432
Async XLA Ops:
  0.0 0.8 %copy-start = (f32[128,128]{1,0:T(8,128)S(1)}, f32[128,128]{1,0:T(8,128)}, u32[]{:S(2)}) copy-start(f32[128,128]{1,0:T(8,128)} %x_hbm.1) | copy-start | bytes 196612

commit v3 on v2

--- a/solution.py
+++ b/solution.py
@@ -147,11 +147,9 @@
 
 def packed_table(count):
     local, ext = (halves(t) for t in filter_tables())
-    summary = halves(np.pad(summary_table(), ((0, 8), (0, 0))))
     comb = halves(combine_table(count))
     return np.concatenate(
         [
-            np.concatenate(summary, axis=1),
             np.concatenate(local, axis=1),
             np.concatenate([ext[0], ext[0], ext[1], ext[1]], axis=1),
             np.concatenate(comb, axis=1).reshape(count * 2 * EXT, count * 16),
@@ -159,7 +157,7 @@
     )
 
 
-LOC_AT, EXT_AT, COMB_AT = 32, 32 + 6 * N, 32 + 12 * N
+LOC_AT, EXT_AT, COMB_AT = 0, 6 * N, 12 * N
 
 
 def split(x):
@@ -174,6 +172,32 @@
 
 def mm(a, b, rhs_lanes=False):
     return dot(a[0], b[0], rhs_lanes) + (dot(a[0], b[1], rhs_lanes) + dot(a[1], b[0], rhs_lanes))
+
+
+def summary_lines():
+    shape = (24, N)
+    row = lax.broadcasted_iota(jnp.int32, shape, 0)
+    n = lax.broadcasted_iota(jnp.int32, shape, 1)
+    part = lax.rem(row, 8)
+    pairs = [(d / s, f / s) for s in SCALES for _, _, d, f in DERICHE_POLES]
+    rate, freq = (
+        jnp.where(
+            part < 4,
+            jnp.where(part < 2, pairs[0][i], pairs[1][i]),
+            jnp.where(part < 6, pairs[2][i], pairs[3][i]),
+        )
+        for i in range(2)
+    )
+    steps = jnp.where(row < 8, N - 1 - n, n).astype(jnp.float32)
+    angle = freq * steps - jnp.where(lax.rem(row, 2) == 1, math.pi / 2, 0.0)
+    square = angle * angle
+    cosine = jnp.full(shape, 1.0 / math.factorial(18), jnp.float32)
+    for k in range(8, -1, -1):
+        cosine = 1.0 / math.factorial(2 * k) - cosine * square
+    wave = jnp.exp(-rate * steps) * cosine
+    cell = jnp.where(row < 12, row - 8, row + N - 16)
+    pick = jnp.where(n == cell, 1.0, 0.0)
+    return jnp.where((row >= 8) & (row < 16), pick, wave)
 
 
 def kernel(
@@ -182,7 +206,6 @@
     tab_hbm,
     o_ref,
     x_ref,
-    m_ref,
     loc_ref,
     ext_ref,
     cv_ref,
@@ -198,8 +221,10 @@
     send_sems,
     recv_sems,
     late_sem,
+    mirror_sem,
+    near_sem,
     row_sem,
-    ok_sems,
+    ok_sem,
 ):
     me_r, me_c = lax.axis_index("row"), lax.axis_index("col")
     part = count // 2
@@ -212,14 +237,14 @@
     def comb_at(pos):
         return tab_hbm.at[pl.ds(pl.multiple_of(COMB_AT + pos * 2 * EXT, 16), 2 * EXT)]
 
-    loads = [
-        load(0, x_hbm, x_ref),
-        load(1, tab_hbm.at[pl.ds(0, 32)], m_ref),
-        load(2, comb_at(me_r), cv_ref),
-        load(3, tab_hbm.at[pl.ds(LOC_AT, 6 * N)], loc_ref),
-        load(4, tab_hbm.at[pl.ds(EXT_AT, 6 * N)], ext_ref),
-        load(5, comb_at(me_c), ch_ref),
+    image, *loads = [
+        load(4, x_hbm, x_ref),
+        load(0, comb_at(me_c), ch_ref),
+        load(1, comb_at(me_r), cv_ref),
+        load(2, tab_hbm.at[pl.ds(LOC_AT, 6 * N)], loc_ref),
+        load(3, tab_hbm.at[pl.ds(EXT_AT, 6 * N)], ext_ref),
     ]
+    image.start()
     for copy in loads:
         copy.start()
 
@@ -243,9 +268,12 @@
         for d in range(1, count):
             greet(barrier, lax.rem(me_r + d, count), me_c)
 
+    mirror = count - 2 - me_c // 2 * 2 + lax.rem(me_c, 2)
+
     @pl.when(half == 1)
     def _():
         pl.semaphore_wait(barrier, part)
+        greet(mirror_sem, me_r, mirror)
         for d in range(part):
             greet(late_sem, me_r, far(d))
 
@@ -261,16 +289,27 @@
             device_id_type=MESH,
         )
 
-    across_near = [message(0, d, near(d), ph_ref, gh_ref) for d in range(1, part)]
-    across_far = [message(0, part + d, far(d), ph_ref, gh_ref) for d in range(part)]
     order = sorted(range(1, count), key=lambda d: -min(d, count - d))
-    down = [message(1, d, lax.rem(me_r + d, count), pv_ref, gv_ref) for d in order]
-    corner = [message(2, d, lax.rem(me_r + d, count), pb_ref, gb_ref) for d in order]
-
-    loads[0].wait()
-    loads[1].wait()
+
+    def send_near():
+        for d in range(1, part):
+            message(0, d, near(d), ph_ref, gh_ref).start()
+
+    def send_far():
+        for d in range(part):
+            message(0, part + d, far(d), ph_ref, gh_ref).start()
+
+    def send_rows(kind, src, dst):
+        for d in order:
+            message(kind, d, lax.rem(me_r + d, count), src, dst).start()
+
+    def received(kind, dst):
+        for d in range(1, count):
+            pltpu.make_async_copy(dst.at[:16], dst.at[:16], recv_sems.at[kind, d]).wait()
+
+    image.wait()
     x = split(x_ref[...])
-    m = (m_ref[:24, :N], m_ref[:24, N:])
+    m = split(summary_lines())
     ph = mm(m, x, True)
     ph_ref[...] = ph
     gh_ref[pl.ds(pl.multiple_of(me_c * 16, 16), 16), :] = ph[:16]
@@ -278,34 +317,27 @@
     pv_ref[...] = pv
     gv_ref[pl.ds(pl.multiple_of(me_r * 16, 16), 16), :] = pv[:16]
 
-    mirror = count - 2 - me_c // 2 * 2 + lax.rem(me_c, 2)
-
     @pl.when(half == 0)
     def _():
         pl.semaphore_wait(barrier, count - 1 + part - 1)
-        for copy in across_near:
-            copy.start()
-        for copy in down:
-            copy.start()
-        pl.semaphore_wait(late_sem, part)
-        greet(ok_sems.at[0], me_r, mirror)
+        send_near()
+        send_rows(1, pv_ref, gv_ref)
+        pl.semaphore_wait(mirror_sem, 1)
         for d in range(1, count):
             greet(row_sem, lax.rem(me_r + d, count), me_c)
-        for copy in across_far:
-            copy.start()
+        pl.semaphore_wait(late_sem, part)
+        greet(near_sem, me_r, mirror)
+        send_far()
         pl.semaphore_wait(row_sem, count - 1)
-        greet(ok_sems.at[1], me_r, mirror)
+        greet(ok_sem, me_r, mirror)
 
     @pl.when(half == 1)
     def _():
-        for copy in across_far:
-            copy.start()
-        pl.semaphore_wait(ok_sems.at[0], 1)
-        for copy in across_near:
-            copy.start()
-        pl.semaphore_wait(ok_sems.at[1], 1)
-        for copy in down:
-            copy.start()
+        send_far()
+        pl.semaphore_wait(near_sem, 1)
+        send_near()
+        pl.semaphore_wait(ok_sem, 1)
+        send_rows(1, pv_ref, gv_ref)
 
     def stacked(v):
         return jnp.concatenate([v[0], v[1], v[0], v[1]], axis=0)
@@ -313,21 +345,18 @@
     def combine(c_ref, g_ref):
         return mm((c_ref[:EXT], c_ref[EXT:]), split(g_ref[...]))
 
-    loads[5].wait()
-    for copy in across_near + across_far:
-        copy.wait_recv()
+    loads[0].wait()
+    received(0, gh_ref)
     lines = combine(ch_ref, gh_ref)
     lines = split(jnp.concatenate([lines, lines], axis=0))
     pb = mm(m, lines, True)
     pb_ref[...] = pb
     gb_ref[pl.ds(pl.multiple_of(me_r * 16, 16), 16), :] = pb[:16]
-    for copy in corner:
-        copy.start()
-    for k in (2, 3, 4):
+    send_rows(2, pb_ref, gb_ref)
+    for k in (1, 2, 3):
         loads[k].wait()
     filtered = dot(loc_ref[...], jnp.concatenate([x[0], x[0]], axis=0)) + dot(loc_ref[:, :N], x[1])
-    for copy in down:
-        copy.wait_recv()
+    received(1, gv_ref)
     filtered = filtered + dot(ext_ref[...], stacked(split(combine(cv_ref, gv_ref))))
     for level in range(2):
         for a in range(3):
@@ -339,8 +368,7 @@
             ) + dot(t[1], loc_ref[wide, :N], True)
 
     carried = mm((loc_ref[:, :N], loc_ref[:, N:]), lines, True)
-    for copy in corner:
-        copy.wait_recv()
+    received(2, gb_ref)
     carried = carried + dot(ext_ref[...], stacked(split(combine(cv_ref, gb_ref))))
 
     high = carried.astype(jnp.bfloat16).astype(jnp.float32)
@@ -355,8 +383,9 @@
             for b in range(3 - a):
                 f = FEATURES.index((a, b))
                 o_ref[level * 6 + f] = full[:, b * N : (b + 1) * N].astype(jnp.bfloat16)
-    for copy in across_near + across_far + down + corner:
-        copy.wait_send()
+    for kind, src in enumerate((ph_ref, pv_ref, pb_ref)):
+        for d in range(1, count):
+            pltpu.make_async_copy(src.at[:16], src.at[:16], send_sems.at[kind, d]).wait()
 
 
 def on_device(count, table, image):
@@ -365,11 +394,10 @@
     return pl.pallas_call(
         functools.partial(kernel, count),
         out_shape=jax.ShapeDtypeStruct((12, N, N), bf16),
-        in_specs=[pl.BlockSpec(memory_space=pl.ANY)] * 2,
+        in_specs=[pl.BlockSpec(memory_space=pltpu.HBM), pl.BlockSpec(memory_space=pl.ANY)],
         out_specs=pl.BlockSpec(memory_space=pltpu.VMEM),
         scratch_shapes=[
             pltpu.VMEM((N, N), f32),
-            pltpu.VMEM((32, 256), bf16),
             pltpu.VMEM((6 * N, 256), bf16),
             pltpu.VMEM((6 * N, 256), bf16),
             pltpu.VMEM((2 * EXT, span), bf16),
@@ -381,17 +409,19 @@
             pltpu.VMEM((span, N), f32),
             pltpu.VMEM((span, N), f32),
             pltpu.VMEM((6, N, 3 * N), f32),
-            pltpu.SemaphoreType.DMA((6,)),
+            pltpu.SemaphoreType.DMA((5,)),
             pltpu.SemaphoreType.DMA((3, count)),
             pltpu.SemaphoreType.DMA((3, count)),
             pltpu.SemaphoreType.REGULAR,
             pltpu.SemaphoreType.REGULAR,
-            pltpu.SemaphoreType.REGULAR((2,)),
+            pltpu.SemaphoreType.REGULAR,
+            pltpu.SemaphoreType.REGULAR,
+            pltpu.SemaphoreType.REGULAR,
         ],
         compiler_params=pltpu.CompilerParams(
             collective_id=0, has_side_effects=True, vmem_limit_bytes=VMEM_LIMIT
         ),
-    )(image, jnp.asarray(table))
+    )(pltpu.with_memory_space_constraint(image, pltpu.HBM), jnp.asarray(table))
 
 
 VMEM_LIMIT = 54000 << 10

time: 23.8 us -> 22.8 us (0.958)
  local copies, waits for them, and re-layouts: 1.59 us -> 0.75 us
    unnamed x3 -> x1, local copies, waits for them, and re-layouts: 1.59 us -> 0.75 us
where the time goes in v3:
time: 22.8 us; the launch traced here: 22.7 us
  Pallas kernels  21.9 us (96%)
  local copies, waits for them, and re-layouts  0.75 us (3%)
    pallas_call x1, Pallas kernels, on_device(): pl.pallas_call(functools.partial(kernel, count), out_shape=jax.ShapeDtype...  21.9 us
    unnamed x1, local copies, waits for them, and re-layouts  0.75 us

profile of v3, /device:TPU:224, one launch (start us, length us, event | category | flops | bytes accessed | tf_op | source)
XLA Modules:
  0.0 22.7 jit_solution(10904238756936508281)
XLA Ops:
  0.0 21.9 %shard_map.28 = bf16[12,128,128]{2,1,0:T(8,128)(2,1)S(1)} custom-call(f32[128,128]{1,0:T(8,128)} %x_hbm.1, bf16[3584,256]{1,0:T(8,128)(2,1)} %constant.2.clone.tab_hbm), custom_call_target="tpu_custom_call" | custom-call | tf_op jit(solution)/shard_map/pallas_call | solution.py:394
  22.0 0.7 %copy.4 = bf16[12,128,128]{2,1,0:T(8,128)(2,1)} copy(bf16[12,128,128]{2,1,0:T(8,128)(2,1)S(1)} %shard_map.28) | data formatting | bytes 786432

commit v4 on v3

--- a/solution.py
+++ b/solution.py
@@ -245,8 +245,9 @@
         load(3, tab_hbm.at[pl.ds(EXT_AT, 6 * N)], ext_ref),
     ]
     image.start()
-    for copy in loads:
-        copy.start()
+
+    early = (0, 1, 2, 3, 4, 5, 6, 7)
+    late = (0, 4, 3, 5, 2, 6, 1, 7)
 
     def near(d):
         return half * part + lax.rem(spot + d, part)
@@ -273,9 +274,12 @@
     @pl.when(half == 1)
     def _():
         pl.semaphore_wait(barrier, part)
+        for d in late:
+            greet(late_sem, me_r, far(d))
         greet(mirror_sem, me_r, mirror)
-        for d in range(part):
-            greet(late_sem, me_r, far(d))
+
+    for copy in loads:
+        copy.start()
 
     def message(kind, k, to, src, dst):
         me = me_c if kind == 0 else me_r
@@ -291,12 +295,12 @@
 
     order = sorted(range(1, count), key=lambda d: -min(d, count - d))
 
-    def send_near():
-        for d in range(1, part):
+    def send_near(ways):
+        for d in ways[1:]:
             message(0, d, near(d), ph_ref, gh_ref).start()
 
-    def send_far():
-        for d in range(part):
+    def send_far(ways):
+        for d in ways:
             message(0, part + d, far(d), ph_ref, gh_ref).start()
 
     def send_rows(kind, src, dst):
@@ -320,27 +324,43 @@
     @pl.when(half == 0)
     def _():
         pl.semaphore_wait(barrier, count - 1 + part - 1)
-        send_near()
+        send_near(early)
         send_rows(1, pv_ref, gv_ref)
         pl.semaphore_wait(mirror_sem, 1)
         for d in range(1, count):
             greet(row_sem, lax.rem(me_r + d, count), me_c)
         pl.semaphore_wait(late_sem, part)
-        greet(near_sem, me_r, mirror)
-        send_far()
+
+        @pl.when(me_c // 2 == 0)
+        def _():
+            greet(near_sem, me_r, me_c + count - 4)
+            greet(near_sem, me_r, me_c + count - 2)
+
+        @pl.when(me_c // 2 == part // 2 - 1)
+        def _():
+            greet(near_sem, me_r, me_c + 2)
+            greet(near_sem, me_r, me_c + 4)
+
+        send_far(late)
         pl.semaphore_wait(row_sem, count - 1)
         greet(ok_sem, me_r, mirror)
 
     @pl.when(half == 1)
     def _():
-        send_far()
+        send_far(early)
         pl.semaphore_wait(near_sem, 1)
-        send_near()
+        send_near(late)
         pl.semaphore_wait(ok_sem, 1)
         send_rows(1, pv_ref, gv_ref)
 
     def stacked(v):
         return jnp.concatenate([v[0], v[1], v[0], v[1]], axis=0)
+
+    def paired(v):
+        high = v.astype(jnp.bfloat16).astype(jnp.float32)
+        lane = lax.broadcasted_iota(jnp.int32, v.shape, 1)
+        pair = jnp.where(lane < EXT, high, v - high).astype(jnp.bfloat16)
+        return jnp.concatenate([pair, pair], axis=1)
 
     def combine(c_ref, g_ref):
         return mm((c_ref[:EXT], c_ref[EXT:]), split(g_ref[...]))
@@ -358,31 +378,29 @@
     filtered = dot(loc_ref[...], jnp.concatenate([x[0], x[0]], axis=0)) + dot(loc_ref[:, :N], x[1])
     received(1, gv_ref)
     filtered = filtered + dot(ext_ref[...], stacked(split(combine(cv_ref, gv_ref))))
+    pair = paired(mm((loc_ref[:, :N], loc_ref[:, N:]), lines, True))
     for level in range(2):
         for a in range(3):
             k = level * 3 + a
+            rows = slice(k * N, (k + 1) * N)
             wide = slice(level * 3 * N, (level * 3 + 3 - a) * N)
-            t = split(filtered[k * N : (k + 1) * N])
-            acc_ref[k, :, : (3 - a) * N] = dot(
-                jnp.concatenate([t[0], t[0]], axis=1), loc_ref[wide], True
-            ) + dot(t[1], loc_ref[wide, :N], True)
-
-    carried = mm((loc_ref[:, :N], loc_ref[:, N:]), lines, True)
+            t = split(filtered[rows])
+            acc_ref[k, :, : (3 - a) * N] = (
+                dot(jnp.concatenate([t[0], t[0]], axis=1), loc_ref[wide], True)
+                + dot(t[1], loc_ref[wide, :N], True)
+                + dot(pair[rows], ext_ref[wide], True)
+            )
+
     received(2, gb_ref)
-    carried = carried + dot(ext_ref[...], stacked(split(combine(cv_ref, gb_ref))))
-
-    high = carried.astype(jnp.bfloat16).astype(jnp.float32)
-    lane = lax.broadcasted_iota(jnp.int32, carried.shape, 1)
-    pair = jnp.where(lane < EXT, high, carried - high).astype(jnp.bfloat16)
-    pair = jnp.concatenate([pair, pair], axis=1)
+    corner = stacked(split(dot(paired(combine(cv_ref, gb_ref)), ext_ref[...], True)))
     for level in range(2):
-        for a in range(3):
-            k = level * 3 + a
-            wide = slice(level * 3 * N, (level * 3 + 3 - a) * N)
-            full = acc_ref[k, :, : (3 - a) * N] + dot(pair[k * N : (k + 1) * N], ext_ref[wide], True)
-            for b in range(3 - a):
-                f = FEATURES.index((a, b))
-                o_ref[level * 6 + f] = full[:, b * N : (b + 1) * N].astype(jnp.bfloat16)
+        for b in range(3):
+            k = level * 3 + b
+            tall = slice(level * 3 * N, (level * 3 + 3 - b) * N)
+            added = dot(ext_ref[tall], corner[:, k * N : (k + 1) * N])
+            for a in range(3 - b):
+                full = acc_ref[level * 3 + a, :, b * N : (b + 1) * N] + added[a * N : (a + 1) * N]
+                o_ref[level * 6 + FEATURES.index((a, b))] = full.astype(jnp.bfloat16)
     for kind, src in enumerate((ph_ref, pv_ref, pb_ref)):
         for d in range(1, count):
             pltpu.make_async_copy(src.at[:16], src.at[:16], send_sems.at[kind, d]).wait()

time: 22.8 us -> 22.6 us (level)
    pallas_call x1, Pallas kernels: 21.9 us -> 21.7 us  [on_device(): pl.pallas_call(functools.partial(kernel, count), out_shape=jax.ShapeDtype...]
where the time goes in v4:
time: 22.6 us; the launch traced here: 22.5 us
  Pallas kernels  21.7 us (96%)
  local copies, waits for them, and re-layouts  0.75 us (3%)
    pallas_call x1, Pallas kernels, on_device(): pl.pallas_call(functools.partial(kernel, count), out_shape=jax.ShapeDtype...  21.7 us
    unnamed x1, local copies, waits for them, and re-layouts  0.75 us

profile of v4, /device:TPU:224, one launch (start us, length us, event | category | flops | bytes accessed | tf_op | source)
XLA Modules:
  0.0 22.5 jit_solution(8498001010920437371)
XLA Ops:
  0.0 21.7 %shard_map.28 = bf16[12,128,128]{2,1,0:T(8,128)(2,1)S(1)} custom-call(f32[128,128]{1,0:T(8,128)} %x_hbm.1, bf16[3584,256]{1,0:T(8,128)(2,1)} %constant.2.clone.tab_hbm), custom_call_target="tpu_custom_call" | custom-call | tf_op jit(solution)/shard_map/pallas_call | solution.py:412
  21.7 0.7 %copy.4 = bf16[12,128,128]{2,1,0:T(8,128)(2,1)} copy(bf16[12,128,128]{2,1,0:T(8,128)(2,1)S(1)} %shard_map.28) | data formatting | bytes 786432

commit v5 on v4

--- a/solution.py
+++ b/solution.py
@@ -325,7 +325,6 @@
     def _():
         pl.semaphore_wait(barrier, count - 1 + part - 1)
         send_near(early)
-        send_rows(1, pv_ref, gv_ref)
         pl.semaphore_wait(mirror_sem, 1)
         for d in range(1, count):
             greet(row_sem, lax.rem(me_r + d, count), me_c)
@@ -342,6 +341,7 @@
             greet(near_sem, me_r, me_c + 4)
 
         send_far(late)
+        send_rows(1, pv_ref, gv_ref)
         pl.semaphore_wait(row_sem, count - 1)
         greet(ok_sem, me_r, mirror)
 

time: 22.6 us -> 22.6 us (level)
  no operation moved by 1% of the time
where the time goes in v5:
time: 22.6 us; the launch traced here: 22.5 us
  Pallas kernels  21.7 us (96%)
  local copies, waits for them, and re-layouts  0.75 us (3%)
    pallas_call x1, Pallas kernels, on_device(): pl.pallas_call(functools.partial(kernel, count), out_shape=jax.ShapeDtype...  21.7 us
    unnamed x1, local copies, waits for them, and re-layouts  0.75 us

profile of v5, /device:TPU:224, one launch (start us, length us, event | category | flops | bytes accessed | tf_op | source)
XLA Modules:
  0.0 22.5 jit_solution(18157562988597747835)
XLA Ops:
  0.0 21.7 %shard_map.28 = bf16[12,128,128]{2,1,0:T(8,128)(2,1)S(1)} custom-call(f32[128,128]{1,0:T(8,128)} %x_hbm.1, bf16[3584,256]{1,0:T(8,128)(2,1)} %constant.2.clone.tab_hbm), custom_call_target="tpu_custom_call" | custom-call | tf_op jit(solution)/shard_map/pallas_call | solution.py:412
  21.7 0.7 %copy.4 = bf16[12,128,128]{2,1,0:T(8,128)(2,1)} copy(bf16[12,128,128]{2,1,0:T(8,128)(2,1)S(1)} %shard_map.28) | data formatting | bytes 786432
